TPU v7x, 128 devices: a whole 4x4x4 slice. The times are simulated.
128 devices in a mesh: samp: 16 (over z_hi, x, core), par: 8 (over y, z_lo).
Axes of the slice: x: 4, y: 4, z: 4 (z_hi: 2, z_lo: 2; z = z_hi * 2 + z_lo), core: 2. Of those that a mesh axis runs over, the one named last changes fastest.
Arguments:
- activations: bfloat16 [10240, 2048], P('samp', 'par'), may hold values from -128 to 128
- signal: bfloat16 [10240, 2], P('samp'), may hold values from -40 to 40
Outputs:
- gram: float32 [10240, 10240], P('samp', 'par')
- panels: float32 [10240, 1280], P('samp', 'par')
All inputs are finite; a program needn't handle non-finite values.
Results may differ from a plain program's by a relative error of at most 0.0022.
Values may be sent and summed in bfloat16 or wider, within the bound.
A program may use at most 128 MiB of HBM per device.

v0:
```python
import jax
import jax.numpy as jnp
from jax import lax
from jax.sharding import PartitionSpec as P

DAMPING = 0.5
EPSILON = 1e-05


def from_root(value, axis, root):
    mine = lax.axis_index(axis) == root
    return lax.psum(jnp.where(mine, value, jnp.zeros_like(value)), axis)


def right_solve(factor, block):
    return jax.scipy.linalg.solve_triangular(factor, block.T, lower=True).T


def first_moment(signal, active):
    return jnp.dot(signal.T, active, preferred_element_type=jnp.float32)


def second_moment(signal_float, active_float):
    products = signal_float[:, :, None] * active_float[:, None, :]
    return jnp.sum(products * products, axis=0)


def normalize(moment_one, moment_two, sample_total, slab_width):
    average = moment_one / sample_total
    column_scale = 1.0 / jnp.sqrt(
        slab_width * (moment_two / sample_total - average * average + EPSILON)
    )
    return (average, column_scale)


def build_rows(signal_float, active_float, average, column_scale):
    centered = signal_float[:, :, None] * active_float[:, None, :] - average[None]
    return (centered * column_scale[None]).astype(jnp.bfloat16)


def per_device(activations, signal):
    signal_float = signal.astype(jnp.float32)
    local_count = activations.shape[0]
    samp_count = lax.axis_size("samp")
    par_count = lax.axis_size("par")
    sample_total = local_count * samp_count
    slab_width = signal.shape[1] * activations.shape[1] * par_count
    active_float = activations.astype(jnp.float32)
    sum_one = first_moment(signal, activations)
    sum_two = second_moment(signal_float, active_float)
    moment_one, moment_two = lax.psum((sum_one, sum_two), "samp")
    average, column_scale = normalize(moment_one, moment_two, sample_total, slab_width)
    local_rows = build_rows(signal_float, active_float, average, column_scale)
    full_rows = lax.all_gather(local_rows, "par", axis=2, tiled=True).reshape(
        local_count, slab_width
    )
    blocks_per = samp_count // par_count
    column = lax.axis_index("par")
    samp_index = lax.axis_index("samp")
    pieces = []
    for offset in range(blocks_per):
        partner = from_root(full_rows, "samp", column * blocks_per + offset)
        pieces.append(
            lax.dot_general(
                full_rows, partner, (((1,), (1,)), ((), ())), preferred_element_type=jnp.float32
            )
        )
    gram_tile = jnp.concatenate(pieces, axis=1)
    global_row = samp_index * local_count + lax.broadcasted_iota(jnp.int32, gram_tile.shape, 0)
    global_col = column * (blocks_per * local_count) + lax.broadcasted_iota(
        jnp.int32, gram_tile.shape, 1
    )
    gram_tile = gram_tile + jnp.where(
        global_row == global_col, jnp.float32(DAMPING), jnp.float32(0.0)
    )
    column_block = from_root(gram_tile, "par", 0)
    identity = jnp.eye(local_count, dtype=jnp.float32)
    first_cols = column_block[:, :local_count]
    second_cols = column_block[:, local_count:]
    factor_one = jnp.linalg.cholesky(jnp.where(samp_index == 0, first_cols, identity))
    factor_one = from_root(factor_one, "samp", 0)
    panel_one = right_solve(factor_one, first_cols)
    partner_panel = from_root(panel_one, "samp", 1)
    update = second_cols - jnp.dot(panel_one, partner_panel.T, precision=lax.Precision.HIGHEST)
    factor_two = jnp.linalg.cholesky(jnp.where(samp_index == 1, update, identity))
    factor_two = from_root(factor_two, "samp", 1)
    panel_two = right_solve(factor_two, update)
    panel_two = jnp.where(samp_index == 0, jnp.float32(0.0), panel_two)
    both_panels = jnp.concatenate([panel_one, panel_two], axis=1)
    own_width = both_panels.shape[1] // par_count
    own_panels = lax.dynamic_slice_in_dim(both_panels, column * own_width, own_width, 1)
    return (gram_tile, own_panels)


def solution(mesh):
    in_specs = (P("samp", "par"), P("samp", None))
    out_specs = (P("samp", "par"), P("samp", "par"))
    return jax.shard_map(
        per_device, mesh=mesh, in_specs=in_specs, out_specs=out_specs, check_vma=False
    )
```

profile of v0, /device:TPU:77, one launch (start us, length us, event | category | flops | bytes accessed | tf_op | source)
XLA Modules:
  0.0 1354.4 jit_solution(4430709151654853441)
XLA Ops:
  10.4 27.9 %all-reduce.1 = (f32[2,256]{1,0:T(2,128)S(1)}, f32[2,256]{1,0:T(2,128)S(1)}) all-reduce(f32[2,256]{1,0:T(2,128)S(1)} %fusion.8, f32[2,256]{1,0:T(2,128)S(1)} %fusion.104), channel_id=1, replica_groups=mesh['samp'=16,'par'=8] {'samp'}, use_global_device_ids=true, to_apply=%region_2.0 | all-reduce | flops 1024 | bytes 8192 | tf_op jit(solution)/shard_map/psum | solution.py:51
  39.5 116.1 %all-gather.2.cloned.1.call-done = bf16[640,2,2048]{0,2,1:T(8,128)(2,1)} async-done(((bf16[640,2,256]{0,2,1:T(8,128)(2,1)}), bf16[640,2,2048]{0,2,1:T(8,128)(2,1)}) %all-gather.2.cloned.1.call-update) | async-done | bytes 5242896 | tf_op jit(solution)/shard_map/all_gather | solution.py:54
  163.0 166.5 %all-reduce.17.cloned.1.call-done = (bf16[640,4096]{0,1:T(8,128)(2,1)}, bf16[640,4096]{0,1:T(8,128)(2,1)}) async-done(((bf16[640,4096]{0,1:T(8,128)(2,1)}, bf16[640,4096]{0,1:T(8,128)(2,1)}), (bf16[640,4096]{0,1:T(8,128)(2,1)}, bf16[640,4096]{0,1:T(8,128)(2,1)})) %all-reduce.17.cloned.1.call-update) | async-done | bytes 10485776 | tf_op jit(solution)/shard_map/psum | solution.py:12
  346.1 152.3 %all-reduce.9.cloned.1.call-done = f32[640,1280]{0,1:T(8,128)} async-done(((f32[640,1280]{0,1:T(8,128)}), f32[640,1280]{0,1:T(8,128)}) %all-reduce.9.cloned.1.call-update) | async-done | bytes 3276816 | tf_op jit(solution)/shard_map/psum | solution.py:12
  504.1 11.7 cholesky.364
  527.2 13.2 cholesky.383
  541.8 11.4 custom-call.35
  554.9 12.3 cholesky.404
  568.7 10.4 custom-call.36
  580.8 11.9 cholesky.423
  603.8 11.7 cholesky.440
  621.5 140.3 %all-reduce.11.cloned.1.call-done = f32[640,640]{1,0:T(8,128)} async-done(((f32[640,640]{1,0:T(8,128)}), f32[640,640]{1,0:T(8,128)}) %all-reduce.11.cloned.1.call-update) | async-done | bytes 1638416 | tf_op jit(solution)/shard_map/psum | solution.py:12
  764.1 13.5 while.4
  777.6 50.6 %custom-call.38 = f32[5,128,128]{1,2,0:T(8,128)} custom-call(f32[5,128,128]{2,1,0:T(8,128)} %get-tuple-element.18), custom_call_target="InvertDiagBlocksLowerTriangular" | custom-call | tf_op jit(solution)/shard_map/jit(_solve_triangular)/triangular_solve | solution.py:16
  842.7 144.0 %all-reduce.13.cloned.1.call-done = f32[640,640]{1,0:T(8,128)} async-done(((f32[640,640]{1,0:T(8,128)}), f32[640,640]{1,0:T(8,128)}) %all-reduce.13.cloned.1.call-update) | async-done | bytes 1638416 | tf_op jit(solution)/shard_map/psum | solution.py:12
  999.0 11.7 cholesky.455
  1024.0 13.2 cholesky.474
  1040.0 11.5 custom-call.40
  1054.0 12.3 cholesky.495
  1080.8 12.1 cholesky.514
  1104.8 11.7 cholesky.531
  1126.3 139.5 %all-reduce.15.cloned.1.call-done = f32[640,640]{1,0:T(8,128)} async-done(((f32[640,640]{1,0:T(8,128)}), f32[640,640]{1,0:T(8,128)}) %all-reduce.15.cloned.1.call-update) | async-done | bytes 1638416 | tf_op jit(solution)/shard_map/psum | solution.py:12
  1268.0 13.2 while.5
  1281.3 50.8 %custom-call.43 = f32[5,128,128]{1,2,0:T(8,128)} custom-call(f32[5,128,128]{2,1,0:T(8,128)} %get-tuple-element.19), custom_call_target="InvertDiagBlocksLowerTriangular" | custom-call | tf_op jit(solution)/shard_map/jit(_solve_triangular)/triangular_solve | solution.py:16
  (184 shorter events, 189.7 us)
Async XLA Ops:
  7.2 148.5 %all-gather.2.cloned.1.call-start = ((), (), s32[]{:S(2)}) async-start(), calls=%async_computation | async-start | bytes 5898240 | tf_op jit(solution)/shard_map/all_gather | solution.py:54
  39.5 290.0 %all-reduce.17.cloned.1.call-start = ((), (), s32[]{:S(2)}) async-start(), calls=%async_computation.5 | async-start | bytes 20971520 | tf_op jit(solution)/shard_map/psum | solution.py:12
  162.9 175.2 %slice-start = ((s8[5242880]{0:T(1024)(128)(4,1)}), s8[1048576]{0:T(1024)(128)(4,1)S(1)}, s32[]{:S(2)}) async-start(s8[5242880]{0:T(1024)(128)(4,1)} %bitcast.139), calls=%async_computation.6 | async-start | bytes 2097152
  163.0 335.4 %all-reduce.9.cloned.1.call-start = ((), (), s32[]{:S(2)}) async-start(), calls=%async_computation.1 | async-start | bytes 6553600 | tf_op jit(solution)/shard_map/psum | solution.py:12
  329.5 8.6 slice-start.1
  329.5 8.7 copy-start.10
  346.1 415.7 %all-reduce.11.cloned.1.call-start = ((), (), s32[]{:S(2)}) async-start(), calls=%async_computation.2 | async-start | bytes 3276800 | tf_op jit(solution)/shard_map/psum | solution.py:12
  502.9 1.2 copy-start.2
  504.1 21.7 %copy-start.3 = (f32[640,640]{1,0:T(8,128)S(1)}, f32[640,640]{1,0:T(8,128)}, u32[]{:S(2)}) copy-start(f32[640,640]{1,0:T(8,128)} %copy-done.2) | copy-start | bytes 4915204
  621.4 365.3 %all-reduce.13.cloned.1.call-start = ((), (), s32[]{:S(2)}) async-start(), calls=%async_computation.3 | async-start | bytes 3276800 | tf_op jit(solution)/shard_map/psum | solution.py:12
  621.5 206.7 %copy-start = (f32[640,640]{1,0:T(8,128)S(1)}, f32[640,640]{1,0:T(8,128)}, u32[]{:S(2)}) copy-start(f32[640,640]{1,0:T(8,128)} %get-tuple-element.55) | copy-start | bytes 4915204
  777.6 50.6 %copy-start.5 = (f32[640,640]{1,0:T(8,128)}, f32[640,640]{1,0:T(8,128)S(1)}, u32[]{:S(2)}) copy-start(f32[640,640]{1,0:T(8,128)S(1)} %get-tuple-element.202) | copy-start | bytes 4915204
  828.2 2.7 copy-start.8
  838.9 1.0 copy-start.6
  842.7 423.1 %all-reduce.15.cloned.1.call-start = ((), (), s32[]{:S(2)}) async-start(), calls=%async_computation.4 | async-start | bytes 3276800 | tf_op jit(solution)/shard_map/psum | solution.py:12
  997.8 1.2 copy-start.1
  1281.3 50.8 %copy-start.4 = (f32[640,640]{1,0:T(8,128)}, f32[640,640]{1,0:T(8,128)S(1)}, u32[]{:S(2)}) copy-start(f32[640,640]{1,0:T(8,128)S(1)} %get-tuple-element.201) | copy-start | bytes 4915204
  1332.0 3.0 copy-start.9
  1343.4 1.0 copy-start.7
Sparse Core Ops, SparseCore 0:
  39.6 115.9 all-gather.1
  163.1 166.4 all-reduce.16
  346.2 152.1 all-reduce.8
  621.6 140.2 all-reduce.10
  842.8 143.8 all-reduce.12
  1121.8 143.8 all-reduce.14
where the time goes:
time: 1370 us; the launch traced here: 1350 us
  waiting for transfers between devices  859 us (63%)
  other arithmetic  342 us (25%)
  matrix products  59.1 us (4%)
  local copies, waits for them, and re-layouts  44.9 us (3%)
  blocking collectives  27.9 us (2%)
  between operations  21.2 us (2%)
    psum x5, waiting for transfers between devices, from_root(): return lax.psum(jnp.where(mine, value, jnp.zeros_like(value)), axis)  743 us
    all_gather x1, waiting for transfers between devices, per_device(): lax.all_gather(local_rows, 'par', axis=2, tiled=True)  116 us
    another operation x19, other arithmetic, per_device(): jnp.linalg.cholesky(jnp.where(samp_index == 1, update, identity))  108 us
    another operation x18, other arithmetic, per_device(): jnp.linalg.cholesky(jnp.where(samp_index == 0, first_cols, identity))  107 us
    another operation x5, other arithmetic, right_solve(): return jax.scipy.linalg.solve_triangular(factor, block.T, lower=True).T  104 us
    another operation x41, local copies, waits for them, and re-layouts, right_solve(): return jax.scipy.linalg.solve_triangular(factor, block.T, lower=True).T  29.2 us
    psum x1, blocking collectives, per_device(): moment_one, moment_two = lax.psum((sum_one, sum_two), 'samp')  27.9 us
  transfers between devices with their start and end apart: 6, of which 6 were waited for; matrix products, arithmetic and copies ran while one was open for 0% of the time, Pallas kernels for 0%

commit v1 on v0

v1 whole, which is shorter than its diff:
```python
import functools

import jax
import jax.numpy as jnp
from jax import lax
from jax.experimental import pallas as pl
from jax.experimental.pallas import tpu as pltpu
from jax.sharding import PartitionSpec as P

DAMPING = 0.5
EPSILON = 1e-05
F32 = jnp.float32
BF = jnp.bfloat16
MESH = pl.DeviceIdType.MESH
ANY = pl.BlockSpec(memory_space=pl.ANY)
VM = pl.BlockSpec(memory_space=pltpu.VMEM)

NX, NY, NZ = 4, 4, 2
NP = 8
NS = 16
ROWS = 640
COLS = 256
WIDE = 2 * ROWS
CH = 4
B = 128


def place():
    s, p = lax.axis_index("samp"), lax.axis_index("par")
    return s, p


class Copies:
    def __init__(self):
        self.sent = []

    def send(self, src, dst, send_sem, recv_sem, s, p, cond=None):
        copy = pltpu.make_async_remote_copy(
            src_ref=src,
            dst_ref=dst,
            send_sem=send_sem,
            recv_sem=recv_sem,
            device_id={"samp": s, "par": p},
            device_id_type=MESH,
        )
        if cond is None:
            copy.start()
        else:
            pl.when(cond)(copy.start)
        self.sent.append((cond, copy))

    def drain(self):
        for cond, copy in self.sent:
            if cond is None:
                copy.wait_send()
            else:
                pl.when(cond)(copy.wait_send)


def arrived(ref, sem):
    pltpu.make_async_copy(ref, ref, sem).wait()


def greet(s, p):
    barrier = pltpu.get_barrier_semaphore()
    for i in range(1, NS):
        pl.semaphore_signal(
            barrier, inc=1, device_id={"samp": lax.rem(s + i, NS), "par": p}, device_id_type=MESH
        )
    for i in range(1, NP):
        pl.semaphore_signal(
            barrier, inc=1, device_id={"samp": s, "par": lax.rem(p + i, NP)}, device_id_type=MESH
        )
    pl.semaphore_wait(barrier, NS + NP - 2)


def first_kernel(
    act, sig, sig_rows, a0, sig_all, stat_all,
    mom, moms, sigs, stat, stats,
    own_sem, one_send, one_recv, two_send, two_recv, core_send, core_recv,
    mom_send, mom_recv, sig_send, sig_recv, stat_send, stat_recv,
):
    s, p = place()
    c, k = lax.rem(s, 2), s // 2
    x, zh = lax.rem(k, NX), k // NX
    y, zl = p // NZ, lax.rem(p, NZ)
    other = s + 1 - 2 * c
    step = ROWS // CH

    def samp_of(zz, xx):
        return 2 * (zz * NX + xx) + c

    def par_of(yy, ll):
        return yy * NZ + ll

    up, down = lax.rem(y + 1, NY), lax.rem(y + NY - 1, NY)
    far, lo = lax.rem(y + 2, NY), 1 - zl
    ahead = jnp.where(c == 0, up, down)
    behind = jnp.where(c == 0, down, up)
    net = Copies()

    def part(q, t):
        return a0.at[c, q, pl.ds(t * step, step), :]

    own_copy = pltpu.make_async_copy(act, a0.at[c, p], own_sem)

    @pl.when(k == 0)
    def _():
        own_copy.start()

    greet(s, p)

    @pl.when(k == 0)
    def _():
        own_copy.wait()

    def stage_own(t):
        @pl.when(k > 0)
        def _():
            arrived(part(p, t), one_recv.at[t])

        net.send(part(p, t), part(p, t), one_send.at[0, t], one_recv.at[t], samp_of(zh, 1), p, x == 0)
        net.send(part(p, t), part(p, t), one_send.at[1, t], one_recv.at[t], samp_of(zh, 3), p, x == 0)
        net.send(part(p, t), part(p, t), one_send.at[2, t], one_recv.at[t], samp_of(1, 0), p, k == 0)
        relay = jnp.logical_or(
            jnp.logical_and(x == 1, c == 0), jnp.logical_and(x == 3, c == 1)
        )
        net.send(part(p, t), part(p, t), one_send.at[3, t], one_recv.at[t], samp_of(zh, 2), p, relay)
        net.send(part(p, t), part(p, t), two_send.at[0, t], two_recv.at[0, t], s, par_of(y, lo))
        net.send(part(p, t), part(p, t), two_send.at[1, t], two_recv.at[1, t], s, par_of(up, zl))
        net.send(part(p, t), part(p, t), two_send.at[2, t], two_recv.at[2, t], s, par_of(down, zl))
        net.send(part(p, t), part(p, t), core_send.at[0, t], core_recv.at[0, t], other, p)

    def stage_near(t):
        q = par_of(y, lo)
        arrived(part(q, t), two_recv.at[0, t])
        net.send(part(q, t), part(q, t), two_send.at[3, t], two_recv.at[3, t], s, par_of(up, zl))
        net.send(part(q, t), part(q, t), two_send.at[4, t], two_recv.at[4, t], s, par_of(down, zl))
        net.send(part(q, t), part(q, t), core_send.at[1, t], core_recv.at[1, t], other, p)
        qu, qd = par_of(down, zl), par_of(up, zl)
        arrived(part(qu, t), two_recv.at[1, t])
        arrived(part(qd, t), two_recv.at[2, t])
        qb = par_of(behind, zl)
        net.send(part(qb, t), part(qb, t), two_send.at[5, t], two_recv.at[5, t], s, par_of(ahead, zl))
        net.send(part(qu, t), part(qu, t), core_send.at[2, t], core_recv.at[2, t], other, p)
        net.send(part(qd, t), part(qd, t), core_send.at[3, t], core_recv.at[3, t], other, p)

    def stage_far(t):
        q = par_of(far, zl)
        arrived(part(q, t), two_recv.at[5, t])
        net.send(part(q, t), part(q, t), two_send.at[6, t], two_recv.at[6, t], s, par_of(y, lo))
        net.send(part(q, t), part(q, t), core_send.at[4, t], core_recv.at[4, t], other, p)
        qu, qd = par_of(down, lo), par_of(up, lo)
        arrived(part(qu, t), two_recv.at[3, t])
        arrived(part(qd, t), two_recv.at[4, t])
        net.send(part(qu, t), part(qu, t), core_send.at[5, t], core_recv.at[5, t], other, p)
        net.send(part(qd, t), part(qd, t), core_send.at[6, t], core_recv.at[6, t], other, p)

    def stage_last(t):
        q = par_of(far, lo)
        arrived(part(q, t), two_recv.at[6, t])
        net.send(part(q, t), part(q, t), core_send.at[7, t], core_recv.at[7, t], other, p)

    for i in range(1, NS):
        net.send(sig_rows, sigs.at[s], sig_send.at[i], sig_recv.at[s], lax.rem(s + i, NS), p)

    @pl.when(k == 0)
    def _():
        pass

    def add(i, sums):
        rows = pl.ds(pl.multiple_of(i * 80, 80), 80)
        a = act[rows, :].astype(F32)
        g = sig[rows, :]
        new = []
        for o in range(2):
            v = g[:, o : o + 1] * a
            new.append(sums[2 * o] + jnp.sum(v.reshape(10, 8, COLS), axis=0))
            new.append(sums[2 * o + 1] + jnp.sum((v * v).reshape(10, 8, COLS), axis=0))
        return tuple(new)

    stage_own(0)
    zero = jnp.zeros((8, COLS), F32)
    sums = lax.fori_loop(0, ROWS // 80, add, (zero,) * 4)
    mom[...] = jnp.concatenate(
        [jnp.sum(v, axis=0, keepdims=True) for v in sums] + [jnp.zeros((4, COLS), F32)], axis=0
    )
    for i in range(1, NS):
        net.send(mom, moms.at[s], mom_send.at[i], mom_recv.at[s], lax.rem(s + i, NS), p)
    moms[s] = mom[...]
    sigs[s] = sig_rows[...]

    for t in range(1, CH + 3):
        if t < CH:
            stage_own(t)
        if t == 1:
            for i in range(1, NS):
                j = lax.rem(s + i, NS)
                arrived(moms.at[j], mom_recv.at[j])
            total = moms[0]
            for j in range(1, NS):
                total = total + moms[j]
            count, width = float(NS * ROWS), float(2 * COLS * NP)
            rows = []
            for o in range(2):
                average = total[2 * o : 2 * o + 1] / count
                second = total[2 * o + 1 : 2 * o + 2] / count
                scale = 1.0 / jnp.sqrt(width * (second - average * average + EPSILON))
                rows += [average, scale]
            stat[...] = jnp.concatenate(rows + [jnp.zeros((4, COLS), F32)], axis=0)
            for i in range(1, NP):
                net.send(stat, stats.at[p], stat_send.at[i], stat_recv.at[p], s, lax.rem(p + i, NP))
            stats[p] = stat[...]
        if 0 <= t - 1 < CH:
            stage_near(t - 1)
        if 0 <= t - 2 < CH:
            stage_far(t - 2)
        if 0 <= t - 3 < CH:
            stage_last(t - 3)

    for i in range(1, NS):
        j = lax.rem(s + i, NS)
        arrived(sigs.at[j], sig_recv.at[j])
    for i in range(1, NP):
        j = lax.rem(p + i, NP)
        arrived(stats.at[j], stat_recv.at[j])
    sig_all[...] = sigs[...]
    stat_all[...] = stats[...]
    order = [
        (y, zl), (y, lo), (down, zl), (up, zl), (far, zl), (down, lo), (up, lo), (far, lo),
    ]
    for t in range(CH):
        for n, (yy, ll) in enumerate(order):
            arrived(a0.at[1 - c, par_of(yy, ll), pl.ds(t * step, step), :], core_recv.at[n, t])
    net.drain()


def gather_first(act, sig, sig_rows):
    dma = pltpu.SemaphoreType.DMA
    return pl.pallas_call(
        first_kernel,
        name="gather_first",
        out_shape=(
            jax.ShapeDtypeStruct((2, NP, ROWS, COLS), BF),
            jax.ShapeDtypeStruct((NS, 8, ROWS), F32),
            jax.ShapeDtypeStruct((NP, 8, COLS), F32),
        ),
        in_specs=[VM, VM, VM],
        out_specs=(ANY, VM, VM),
        scratch_shapes=[
            pltpu.VMEM((8, COLS), F32),
            pltpu.VMEM((NS, 8, COLS), F32),
            pltpu.VMEM((NS, 8, ROWS), F32),
            pltpu.VMEM((8, COLS), F32),
            pltpu.VMEM((NP, 8, COLS), F32),
            dma, dma((4, CH)), dma((CH,)), dma((7, CH)), dma((7, CH)), dma((8, CH)), dma((8, CH)),
            dma((NS,)), dma((NS,)), dma((NS,)), dma((NS,)), dma((NP,)), dma((NP,)),
        ],
        compiler_params=pltpu.CompilerParams(collective_id=0, has_side_effects=True),
    )(act, sig, sig_rows)


def rest_kernel(
    act, ar, ac, kbuf,
    own_sem, row_send, row_recv, col_send, col_recv, two_send, two_recv, core_send, core_recv,
):
    s, p = place()
    c, k = lax.rem(s, 2), s // 2
    other = s + 1 - 2 * c
    net = Copies()
    own = [
        pltpu.make_async_copy(act, ar.at[p], own_sem.at[0]),
        pltpu.make_async_copy(act, kbuf.at[k], own_sem.at[1]),
    ]
    for copy in own:
        copy.start()
    greet(s, p)
    for i in range(1, NP):
        to = lax.rem(k + i, NP)
        net.send(act, kbuf.at[k], col_send.at[i], col_recv.at[k], 2 * to + c, p)
    for i in range(1, NP):
        net.send(act, ar.at[p], row_send.at[i], row_recv.at[p], s, lax.rem(p + i, NP))
    for copy in own:
        copy.wait()
    for i in range(1, NP):
        j = lax.rem(k + i, NP)
        arrived(kbuf.at[j], col_recv.at[j])
    mine = pltpu.make_async_copy(kbuf.at[p], ac.at[c, p], own_sem.at[2])
    mine.start()
    for i in range(1, NP):
        to = lax.rem(p + i, NP)
        net.send(kbuf.at[to], ac.at[c, p], two_send.at[i], two_recv.at[p], s, to)
    mine.wait()
    for i in range(NP):
        j = lax.rem(p + i, NP)
        if i:
            arrived(ac.at[c, j], two_recv.at[j])
        net.send(ac.at[c, j], ac.at[c, j], core_send.at[i], core_recv.at[j], other, p)
    for i in range(1, NP):
        j = lax.rem(p + i, NP)
        arrived(ar.at[j], row_recv.at[j])
    for j in range(NP):
        arrived(ac.at[1 - c, j], core_recv.at[j])
    net.drain()


def gather_rest(act):
    dma = pltpu.SemaphoreType.DMA
    return pl.pallas_call(
        rest_kernel,
        name="gather_rest",
        out_shape=(
            jax.ShapeDtypeStruct((NP, ROWS, COLS), BF),
            jax.ShapeDtypeStruct((2, NP, ROWS, COLS), BF),
        ),
        in_specs=[VM],
        out_specs=(ANY, ANY),
        scratch_shapes=[
            pltpu.VMEM((NP, ROWS, COLS), BF),
            dma((3,)), dma((NP,)), dma((NP,)), dma((NP,)), dma((NP,)), dma((NP,)), dma((NP,)),
            dma((NP,)), dma((NP,)),
        ],
        compiler_params=pltpu.CompilerParams(collective_id=1, has_side_effects=True),
    )(act)


def split(v):
    hi = v.astype(BF)
    return hi, (v - hi.astype(F32)).astype(BF)


def dot3(a, b, ca, cb):
    dims = (((ca,), (cb,)), ((), ()))

    def one(u, v):
        return lax.dot_general(u, v, dims, preferred_element_type=F32)

    return one(a[0], b[1]) + one(a[1], b[0]) + one(a[0], b[0])


def dot1(a, b):
    return lax.dot_general(a, b, (((1,), (1,)), ((), ())), preferred_element_type=F32)


def row(v, i):
    return jnp.broadcast_to(v[i : i + 1, :], (8, B))


def lane(v, i):
    return jnp.broadcast_to(v[:, i : i + 1], (8, B))


def leaf(tiles, eye, sub):
    out = []
    for m in range(len(tiles)):
        top, unit = tiles[m], eye[m]
        cols = [[lane(tiles[i], 8 * m + b) for b in range(8)] for i in range(m, len(tiles))]
        scale, factors = None, []
        for k in range(8):
            r = lax.rsqrt(row(cols[0][k], k))
            inv = r * r
            scale = r if scale is None else jnp.where(sub == k, r, scale)
            pivots = [row(cols[0][k], b) for b in range(k + 1, 8)]
            f = [v[k] * inv for v in cols]
            for v, g in zip(cols, f):
                for b in range(k + 1, 8):
                    v[b] = v[b] - g * pivots[b - k - 1]
            if k < 7:
                below = jnp.where(sub > k, f[0], 0.0)
                top = top - below * row(top, k)
                unit = unit - below * row(unit, k)
            factors.append(f[1:])
        for n, i in enumerate(range(m + 1, len(tiles))):
            da = functools.reduce(jnp.add, [factors[k][n] * row(top, k) for k in range(8)])
            du = functools.reduce(jnp.add, [factors[k][n] * row(unit, k) for k in range(8)])
            tiles[i] = tiles[i] - da
            eye[i] = eye[i] - du
        out.append(unit * scale)
    return out


def factor_inverse(z, inv_block):
    n = z.shape[0]
    nb = n // B
    sub = lax.broadcasted_iota(jnp.int32, (8, B), 0)
    ln = lax.broadcasted_iota(jnp.int32, (8, B), 1)

    def body(j, carry):
        j0 = pl.multiple_of(j * B, B)
        here = pl.ds(j0, B)
        tiles = [z[pl.ds(pl.multiple_of(j0 + 8 * i, 8), 8), here] for i in range(B // 8)]
        eye = [jnp.where(ln == sub + 8 * i, 1.0, 0.0).astype(F32) for i in range(B // 8)]
        for i, v in enumerate(leaf(tiles, eye, sub)):
            inv_block[8 * i : 8 * i + 8, :] = v
        w = inv_block[...]
        z[here, :] = dot3(split(w), split(z[here, :]), 1, 0)
        z[here, here] = w
        for jj in range(nb - 1):

            @pl.when(j == jj)
            def _():
                y = split(z[jj * B : jj * B + B, :])
                low = (jj + 1) * B
                z[low:, jj * B : low] = jnp.zeros((n - low, B), F32)
                for t in range(jj + 1, nb):
                    rows = slice(t * B, t * B + B)
                    z[rows, :] = z[rows, :] - dot3((y[0][:, rows], y[1][:, rows]), y, 0, 0)

        return carry

    lax.fori_loop(0, nb, body, 0)


def fill(dst, base, act, sig_cols, stat):
    a = act.astype(F32)
    for o in range(2):
        v = sig_cols[:, o : o + 1] * a
        v = (v - stat[2 * o : 2 * o + 1]) * stat[2 * o + 1 : 2 * o + 2]
        dst[base : base + ROWS, o * COLS : (o + 1) * COLS] = v.astype(BF)


def cols_of(rows):
    return jnp.transpose(rows)


def factor_kernel(a0, sig_all, stat_all, w_out, z, jac, sig_cols, inv_block, sem):
    q = pl.program_id(0)

    @pl.when(q == 0)
    def _():
        for h in range(2):
            sig_cols[h] = cols_of(sig_all[h])
        z[...] = jnp.zeros_like(z)

    for h in range(2):
        fill(jac, h * ROWS, a0[h, 0], sig_cols[h], stat_all[0])
    for r in range(WIDE // COLS):
        rows = slice(r * COLS, (r + 1) * COLS)
        z[rows, r * COLS :] += dot1(jac[rows, :], jac[r * COLS :, :])

    @pl.when(q == NP - 1)
    def _():
        for r in range(WIDE // B):
            rows = slice(r * B, (r + 1) * B)
            i = lax.broadcasted_iota(jnp.int32, (B, B), 0)
            j = lax.broadcasted_iota(jnp.int32, (B, B), 1)
            z[rows, rows] += jnp.where(i == j, DAMPING, 0.0).astype(F32)
        factor_inverse(z, inv_block)
        copy = pltpu.make_async_copy(z, w_out, sem)
        copy.start()
        copy.wait()


def factor(a0, sig_all, stat_all):
    return pl.pallas_call(
        factor_kernel,
        name="factor",
        grid=(NP,),
        out_shape=jax.ShapeDtypeStruct((WIDE, WIDE), F32),
        in_specs=[
            pl.BlockSpec((2, 1, ROWS, COLS), lambda q: (0, q, 0, 0)),
            pl.BlockSpec((2, 8, ROWS), lambda q: (0, 0, 0)),
            pl.BlockSpec((1, 8, COLS), lambda q: (q, 0, 0)),
        ],
        out_specs=ANY,
        scratch_shapes=[
            pltpu.VMEM((WIDE, WIDE), F32),
            pltpu.VMEM((WIDE, 2 * COLS), BF),
            pltpu.VMEM((2, ROWS, 8), F32),
            pltpu.VMEM((B, B), F32),
            pltpu.SemaphoreType.DMA,
        ],
        compiler_params=pltpu.CompilerParams(vmem_limit_bytes=56 * 2**20),
    )(a0, sig_all, stat_all)


def final_kernel(
    ar, ac, a0, sig_all, stat_all, w_all, gram, panel,
    lead, jr, jc, j0, sig_r, sig_c, sig_0, w, sem,
):
    q = pl.program_id(0)
    s, p = place()
    width = WIDE // NP

    fetch = pltpu.make_async_copy(
        w_all.at[pl.ds(pl.multiple_of(p * width, 8), width), :], w, sem
    )

    @pl.when(q == 0)
    def _():
        fetch.start()
        sig_r[...] = cols_of(sig_all[s])
        for h in range(2):
            sig_c[h] = cols_of(sig_all[2 * p + h])
            sig_0[h] = cols_of(sig_all[h])
        gram[...] = jnp.zeros_like(gram)
        lead[...] = jnp.zeros_like(lead)

    stat = stat_all[0]
    fill(jr, 0, ar[0], sig_r, stat)
    for h in range(2):
        fill(jc, h * ROWS, ac[h, 0], sig_c[h], stat)
        fill(j0, h * ROWS, a0[h, 0], sig_0[h], stat)
    gram[...] += dot1(jr[...], jc[...])
    lead[...] += dot1(jr[...], j0[...])

    @pl.when(q == NP - 1)
    def _():
        i = lax.broadcasted_iota(jnp.int32, (ROWS, WIDE), 0) + s * ROWS
        j = lax.broadcasted_iota(jnp.int32, (ROWS, WIDE), 1)
        gram[...] += jnp.where(i == j + p * WIDE, DAMPING, 0.0).astype(F32)
        g = lead[...] + jnp.where(i == j, DAMPING, 0.0).astype(F32)
        fetch.wait()
        wi = lax.broadcasted_iota(jnp.int32, (width, WIDE), 0) + p * width
        wj = lax.broadcasted_iota(jnp.int32, (width, WIDE), 1)
        low = jnp.where(wj <= wi, w[...], 0.0)
        out = dot3(split(g), split(low), 1, 1)
        skip = jnp.logical_and(s == 0, p >= NP // 2)
        panel[...] = jnp.where(skip, 0.0, out)


def finish(ar, ac, a0, sig_all, stat_all, w_all):
    whole = lambda *shape: pl.BlockSpec(shape, lambda q: (0,) * len(shape))
    return pl.pallas_call(
        final_kernel,
        name="finish",
        grid=(NP,),
        out_shape=(
            jax.ShapeDtypeStruct((ROWS, WIDE), F32),
            jax.ShapeDtypeStruct((ROWS, WIDE // NP), F32),
        ),
        in_specs=[
            pl.BlockSpec((1, ROWS, COLS), lambda q: (q, 0, 0)),
            pl.BlockSpec((2, 1, ROWS, COLS), lambda q: (0, q, 0, 0)),
            pl.BlockSpec((2, 1, ROWS, COLS), lambda q: (0, q, 0, 0)),
            whole(NS, 8, ROWS),
            pl.BlockSpec((1, 8, COLS), lambda q: (q, 0, 0)),
            ANY,
        ],
        out_specs=(whole(ROWS, WIDE), whole(ROWS, WIDE // NP)),
        scratch_shapes=[
            pltpu.VMEM((ROWS, WIDE), F32),
            pltpu.VMEM((ROWS, 2 * COLS), BF),
            pltpu.VMEM((WIDE, 2 * COLS), BF),
            pltpu.VMEM((WIDE, 2 * COLS), BF),
            pltpu.VMEM((ROWS, 8), F32),
            pltpu.VMEM((2, ROWS, 8), F32),
            pltpu.VMEM((2, ROWS, 8), F32),
            pltpu.VMEM((WIDE // NP, WIDE), F32),
            pltpu.SemaphoreType.DMA,
        ],
        compiler_params=pltpu.CompilerParams(vmem_limit_bytes=56 * 2**20),
    )(ar, ac, a0, sig_all, stat_all, w_all)


def per_device(activations, signal):
    sig = signal.astype(F32)
    sig_rows = jnp.pad(sig.T, ((0, 6), (0, 0)))
    a0, sig_all, stat_all = gather_first(activations, sig, sig_rows)
    ar, ac = gather_rest(activations)
    w = factor(a0, sig_all, stat_all)
    return finish(ar, ac, a0, sig_all, stat_all, w)


def solution(mesh):
    return jax.shard_map(
        per_device,
        mesh=mesh,
        in_specs=(P("samp", "par"), P("samp", None)),
        out_specs=(P("samp", "par"), P("samp", "par")),
        check_vma=False,
    )
```

time: 1370 us -> 283 us (0.21)
  the two profiles are of different devices: /device:TPU:77 before, /device:TPU:35 now
where the time goes in v1:
time: 283 us
  Pallas kernels  278 us (98%)
  local copies, waits for them, and re-layouts  4.23 us (1%)
    pallas_call x1, Pallas kernels, gather_rest(): pl.pallas_call(rest_kernel, name='gather_rest', out_shape=(jax.ShapeDtype...  118 us
    pallas_call x1, Pallas kernels, factor(): pl.pallas_call(factor_kernel, name='factor', grid=(NP,), out_shape=jax.Sh...  76.8 us
    pallas_call x1, Pallas kernels, gather_first(): pl.pallas_call(first_kernel, name='gather_first', out_shape=(jax.ShapeDty...  58.6 us
    pallas_call x1, Pallas kernels, finish(): pl.pallas_call(final_kernel, name='finish', grid=(NP,), out_shape=(jax.Sh...  24.2 us

profile of v1, /device:TPU:35, one launch (start us, length us, event | category | flops | bytes accessed | tf_op | source)
XLA Modules:
  0.0 283.2 jit_solution(4859863448276239685)
XLA Ops:
  0.6 0.7 convert_bitcast_fusion
  1.3 0.6 pad.4.sig_rows
  1.9 1.6 copy.4.sig
  3.5 58.6 %gather_first.1 = (bf16[2,8,640,256]{3,2,1,0:T(8,128)(2,1)}, f32[16,8,640]{2,1,0:T(8,128)}, f32[8,8,256]{2,1,0:T(8,128)}) custom-call(bf16[640,256]{1,0:T(8,128)(2,1)} %act.3, f32[640,2]{1,0:T(8,128)} %copy.4.sig, f32[8,640]{1,0:T(8,128)} %pad.4.sig_rows), custom_call_target="tpu_custom_call" | custom-call | tf_op jit(solution)/shard_map/gather_first/pallas_call | solution.py:240
  62.1 76.8 %factor.1.w_all = f32[1280,1280]{1,0:T(8,128)} custom-call(bf16[2,8,640,256]{3,2,1,0:T(8,128)(2,1)} %get-tuple-element.9.a0, f32[16,8,640]{2,1,0:T(8,128)} %get-tuple-element.10.sig_all, f32[8,8,256]{2,1,0:T(8,128)} %get-tuple-element.11.stat_all), custom_call_target="tpu_custom_call" | custom-call | tf_op jit(solution)/shard_map/factor/pallas_call | solution.py:455
  139.0 118.0 %gather_rest.1 = (bf16[8,640,256]{2,1,0:T(8,128)(2,1)}, bf16[2,8,640,256]{3,2,1,0:T(8,128)(2,1)}) custom-call(bf16[640,256]{1,0:T(8,128)(2,1)} %act.3), custom_call_target="tpu_custom_call" | custom-call | tf_op jit(solution)/shard_map/gather_rest/pallas_call | solution.py:309
  256.9 24.2 %finish.1 = (f32[640,1280]{1,0:T(8,128)}, f32[640,160]{1,0:T(8,128)}) custom-call(bf16[8,640,256]{2,1,0:T(8,128)(2,1)} %get-tuple-element.7.ar, bf16[2,8,640,256]{3,2,1,0:T(8,128)(2,1)} %get-tuple-element.8.ac, bf16[2,8,640,256]{3,2,1,0:T(8,128)(2,1)} %get-tuple-element.9.a0, f32[16,8,640]{2,1,0:T(8,128)} %get-tuple-element.10.sig_all, ...), custom_call_target="tpu_custom_call" | custom-call | tf_op jit(solution)/shard_map/finish/pallas_call | solution.py:524
  281.1 2.0 copy.5

commit v2 on v1

--- a/solution.py
+++ b/solution.py
@@ -260,68 +260,71 @@
     )(act, sig, sig_rows)
 
 
-def rest_kernel(
-    act, ar, ac, kbuf,
-    own_sem, row_send, row_recv, col_send, col_recv, two_send, two_recv, core_send, core_recv,
-):
-    s, p = place()
-    c, k = lax.rem(s, 2), s // 2
-    other = s + 1 - 2 * c
-    net = Copies()
-    own = [
-        pltpu.make_async_copy(act, ar.at[p], own_sem.at[0]),
-        pltpu.make_async_copy(act, kbuf.at[k], own_sem.at[1]),
-    ]
-    for copy in own:
-        copy.start()
-    greet(s, p)
-    for i in range(1, NP):
-        to = lax.rem(k + i, NP)
-        net.send(act, kbuf.at[k], col_send.at[i], col_recv.at[k], 2 * to + c, p)
-    for i in range(1, NP):
-        net.send(act, ar.at[p], row_send.at[i], row_recv.at[p], s, lax.rem(p + i, NP))
-    for copy in own:
-        copy.wait()
-    for i in range(1, NP):
-        j = lax.rem(k + i, NP)
-        arrived(kbuf.at[j], col_recv.at[j])
-    mine = pltpu.make_async_copy(kbuf.at[p], ac.at[c, p], own_sem.at[2])
-    mine.start()
-    for i in range(1, NP):
-        to = lax.rem(p + i, NP)
-        net.send(kbuf.at[to], ac.at[c, p], two_send.at[i], two_recv.at[p], s, to)
-    mine.wait()
-    for i in range(NP):
-        j = lax.rem(p + i, NP)
-        if i:
-            arrived(ac.at[c, j], two_recv.at[j])
-        net.send(ac.at[c, j], ac.at[c, j], core_send.at[i], core_recv.at[j], other, p)
-    for i in range(1, NP):
-        j = lax.rem(p + i, NP)
-        arrived(ar.at[j], row_recv.at[j])
-    for j in range(NP):
-        arrived(ac.at[1 - c, j], core_recv.at[j])
-    net.drain()
-
-
-def gather_rest(act):
-    dma = pltpu.SemaphoreType.DMA
-    return pl.pallas_call(
-        rest_kernel,
-        name="gather_rest",
-        out_shape=(
-            jax.ShapeDtypeStruct((NP, ROWS, COLS), BF),
-            jax.ShapeDtypeStruct((2, NP, ROWS, COLS), BF),
-        ),
-        in_specs=[VM],
-        out_specs=(ANY, ANY),
-        scratch_shapes=[
-            pltpu.VMEM((NP, ROWS, COLS), BF),
-            dma((3,)), dma((NP,)), dma((NP,)), dma((NP,)), dma((NP,)), dma((NP,)), dma((NP,)),
-            dma((NP,)), dma((NP,)),
-        ],
-        compiler_params=pltpu.CompilerParams(collective_id=1, has_side_effects=True),
-    )(act)
+class Rest:
+    def __init__(self, act, ar, ac, kbuf, sems):
+        (own_sem, row_send, row_recv, col_send, col_recv, two_send, two_recv, core_send, core_recv) = sems
+        s, p = place()
+        c, k = lax.rem(s, 2), s // 2
+        other = s + 1 - 2 * c
+        self.own = [
+            pltpu.make_async_copy(act, ar.at[p], own_sem.at[0]),
+            pltpu.make_async_copy(act, kbuf.at[k], own_sem.at[1]),
+            pltpu.make_async_copy(kbuf.at[p], ac.at[c, p], own_sem.at[2]),
+        ]
+        self.col, self.row, self.two, self.core = [], [], [], []
+        self.col_in, self.row_in, self.two_in, self.core_in = [], [], [], []
+        for i in range(1, NP):
+            to, on = lax.rem(k + i, NP), lax.rem(p + i, NP)
+            self.col.append(far_copy(act, kbuf.at[k], col_send.at[i], col_recv.at[k], 2 * to + c, p))
+            self.row.append(far_copy(act, ar.at[p], row_send.at[i], row_recv.at[p], s, on))
+            self.two.append(far_copy(kbuf.at[on], ac.at[c, p], two_send.at[i], two_recv.at[p], s, on))
+            self.col_in.append((kbuf.at[to], col_recv.at[to]))
+            self.row_in.append((ar.at[on], row_recv.at[on]))
+            self.two_in.append((ac.at[c, on], two_recv.at[on]))
+        for i in range(NP):
+            on = lax.rem(p + i, NP)
+            self.core.append(far_copy(ac.at[c, on], ac.at[c, on], core_send.at[i], core_recv.at[on], other, p))
+            self.core_in.append((ac.at[1 - c, i], core_recv.at[i]))
+
+    def begin(self):
+        s, p = place()
+        self.own[0].start()
+        self.own[1].start()
+        greet(s, p)
+        for copy in self.col + self.row:
+            copy.start()
+
+    def second(self):
+        self.own[0].wait()
+        self.own[1].wait()
+        for ref, sem in self.col_in:
+            arrived(ref, sem)
+        for copy in self.two + [self.own[2]]:
+            copy.start()
+
+    def third(self):
+        self.own[2].wait()
+        self.core[0].start()
+        for (ref, sem), copy in zip(self.two_in, self.core[1:]):
+            arrived(ref, sem)
+            copy.start()
+
+    def end(self):
+        for ref, sem in self.row_in + self.core_in:
+            arrived(ref, sem)
+        for copy in self.col + self.row + self.two + self.core:
+            copy.wait_send()
+
+
+def far_copy(src, dst, send_sem, recv_sem, s, p):
+    return pltpu.make_async_remote_copy(
+        src_ref=src,
+        dst_ref=dst,
+        send_sem=send_sem,
+        recv_sem=recv_sem,
+        device_id={"samp": s, "par": p},
+        device_id_type=MESH,
+    )
 
 
 def split(v):
@@ -379,13 +382,14 @@
     return out
 
 
-def factor_inverse(z, inv_block):
+def factor_inverse(z, inv_block, between):
     n = z.shape[0]
     nb = n // B
     sub = lax.broadcasted_iota(jnp.int32, (8, B), 0)
     ln = lax.broadcasted_iota(jnp.int32, (8, B), 1)
 
     def body(j, carry):
+        between(j)
         j0 = pl.multiple_of(j * B, B)
         here = pl.ds(j0, B)
         tiles = [z[pl.ds(pl.multiple_of(j0 + 8 * i, 8), 8), here] for i in range(B // 8)]
@@ -423,8 +427,12 @@
     return jnp.transpose(rows)
 
 
-def factor_kernel(a0, sig_all, stat_all, w_out, z, jac, sig_cols, inv_block, sem):
+def factor_kernel(
+    a0, sig_all, stat_all, act, w_out, ar, ac, z, jac, sig_cols, inv_block, kbuf, sem, *sems
+):
     q = pl.program_id(0)
+    rest = Rest(act, ar, ac, kbuf, sems)
+    pl.when(q == 0)(rest.begin)
 
     @pl.when(q == 0)
     def _():
@@ -445,33 +453,47 @@
             i = lax.broadcasted_iota(jnp.int32, (B, B), 0)
             j = lax.broadcasted_iota(jnp.int32, (B, B), 1)
             z[rows, rows] += jnp.where(i == j, DAMPING, 0.0).astype(F32)
-        factor_inverse(z, inv_block)
+        def between(j):
+            pl.when(j == 1)(rest.second)
+            pl.when(j == 8)(rest.third)
+
+        factor_inverse(z, inv_block, between)
         copy = pltpu.make_async_copy(z, w_out, sem)
         copy.start()
+        rest.end()
         copy.wait()
 
 
-def factor(a0, sig_all, stat_all):
+def factor(a0, sig_all, stat_all, act):
+    dma = pltpu.SemaphoreType.DMA
     return pl.pallas_call(
         factor_kernel,
         name="factor",
         grid=(NP,),
-        out_shape=jax.ShapeDtypeStruct((WIDE, WIDE), F32),
+        out_shape=(
+            jax.ShapeDtypeStruct((WIDE, WIDE), F32),
+            jax.ShapeDtypeStruct((NP, ROWS, COLS), BF),
+            jax.ShapeDtypeStruct((2, NP, ROWS, COLS), BF),
+        ),
         in_specs=[
             pl.BlockSpec((2, 1, ROWS, COLS), lambda q: (0, q, 0, 0)),
             pl.BlockSpec((2, 8, ROWS), lambda q: (0, 0, 0)),
             pl.BlockSpec((1, 8, COLS), lambda q: (q, 0, 0)),
+            VM,
         ],
-        out_specs=ANY,
+        out_specs=(ANY, ANY, ANY),
         scratch_shapes=[
             pltpu.VMEM((WIDE, WIDE), F32),
             pltpu.VMEM((WIDE, 2 * COLS), BF),
             pltpu.VMEM((2, ROWS, 8), F32),
             pltpu.VMEM((B, B), F32),
-            pltpu.SemaphoreType.DMA,
+            pltpu.VMEM((NP, ROWS, COLS), BF),
+            dma, dma((3,)), *[dma((NP,))] * 8,
         ],
-        compiler_params=pltpu.CompilerParams(vmem_limit_bytes=56 * 2**20),
-    )(a0, sig_all, stat_all)
+        compiler_params=pltpu.CompilerParams(
+            collective_id=1, has_side_effects=True, vmem_limit_bytes=56 * 2**20
+        ),
+    )(a0, sig_all, stat_all, act)
 
 
 def final_kernel(
@@ -557,8 +579,7 @@
     sig = signal.astype(F32)
     sig_rows = jnp.pad(sig.T, ((0, 6), (0, 0)))
     a0, sig_all, stat_all = gather_first(activations, sig, sig_rows)
-    ar, ac = gather_rest(activations)
-    w = factor(a0, sig_all, stat_all)
+    w, ar, ac = factor(a0, sig_all, stat_all, activations)
     return finish(ar, ac, a0, sig_all, stat_all, w)
 
 

time: 283 us -> 229 us (0.81)
  the two profiles are of different devices: /device:TPU:35 before, /device:TPU:44 now
where the time goes in v2:
time: 229 us
  Pallas kernels  224 us (98%)
  local copies, waits for them, and re-layouts  4.23 us (2%)
    pallas_call x1, Pallas kernels, factor(): pl.pallas_call(factor_kernel, name='factor', grid=(NP,), out_shape=(jax.S...  140 us
    pallas_call x1, Pallas kernels, gather_first(): pl.pallas_call(first_kernel, name='gather_first', out_shape=(jax.ShapeDty...  59.4 us
    pallas_call x1, Pallas kernels, finish(): pl.pallas_call(final_kernel, name='finish', grid=(NP,), out_shape=(jax.Sh...  24.2 us

profile of v2, /device:TPU:44, one launch (start us, length us, event | category | flops | bytes accessed | tf_op | source)
XLA Modules:
  0.0 229.1 jit_solution(5507909372556681337)
XLA Ops:
  0.6 0.7 convert_bitcast_fusion
  1.3 0.6 pad.4.sig_rows
  1.9 1.6 copy.4.sig
  3.5 59.4 %gather_first.1 = (bf16[2,8,640,256]{3,2,1,0:T(8,128)(2,1)}, f32[16,8,640]{2,1,0:T(8,128)}, f32[8,8,256]{2,1,0:T(8,128)}) custom-call(bf16[640,256]{1,0:T(8,128)(2,1)} %act.3, f32[640,2]{1,0:T(8,128)} %copy.4.sig, f32[8,640]{1,0:T(8,128)} %pad.4.sig_rows), custom_call_target="tpu_custom_call" | custom-call | tf_op jit(solution)/shard_map/gather_first/pallas_call | solution.py:240
  62.9 140.0 %factor.1 = (f32[1280,1280]{1,0:T(8,128)}, bf16[8,640,256]{2,1,0:T(8,128)(2,1)}, bf16[2,8,640,256]{3,2,1,0:T(8,128)(2,1)}) custom-call(bf16[2,8,640,256]{3,2,1,0:T(8,128)(2,1)} %get-tuple-element.8.a0, f32[16,8,640]{2,1,0:T(8,128)} %get-tuple-element.9.sig_all, f32[8,8,256]{2,1,0:T(8,128)} %get-tuple-element.10.stat_all, bf16[640,256]{1,0:T(8,128)(2,1)} %act.3), custom_call_target="tpu_custom_call" | custom-call | tf_op jit(solution)/shard_map/factor/pallas_call | solution.py:469
  202.9 24.2 %finish.1 = (f32[640,1280]{1,0:T(8,128)}, f32[640,160]{1,0:T(8,128)}) custom-call(bf16[8,640,256]{2,1,0:T(8,128)(2,1)} %get-tuple-element.11.ar, bf16[2,8,640,256]{3,2,1,0:T(8,128)(2,1)} %get-tuple-element.12.ac, bf16[2,8,640,256]{3,2,1,0:T(8,128)(2,1)} %get-tuple-element.8.a0, f32[16,8,640]{2,1,0:T(8,128)} %get-tuple-element.9.sig_all, ...), custom_call_target="tpu_custom_call" | custom-call | tf_op jit(solution)/shard_map/finish/pallas_call | solution.py:546
  227.1 2.0 copy.5

commit v3 on v0

v3 whole, which is shorter than its diff:
```python
import functools

import jax
import jax.numpy as jnp
from jax import lax
from jax.experimental import pallas as pl
from jax.experimental.pallas import tpu as pltpu
from jax.sharding import PartitionSpec as P

DAMPING = 0.5
EPSILON = 1e-05
F32 = jnp.float32
BF = jnp.bfloat16
MESH = pl.DeviceIdType.MESH
ANY = pl.BlockSpec(memory_space=pl.ANY)
VM = pl.BlockSpec(memory_space=pltpu.VMEM)

NX, NY, NZ = 4, 4, 2
NP = 8
NS = 16
ROWS = 640
COLS = 256
WIDE = 2 * ROWS
CH = 4
BCH = 2
NB = 10
B = 128


def place():
    s, p = lax.axis_index("samp"), lax.axis_index("par")
    return s, p


class Copies:
    def __init__(self):
        self.sent = []

    def send(self, src, dst, send_sem, recv_sem, s, p, cond=None):
        copy = pltpu.make_async_remote_copy(
            src_ref=src,
            dst_ref=dst,
            send_sem=send_sem,
            recv_sem=recv_sem,
            device_id={"samp": s, "par": p},
            device_id_type=MESH,
        )
        if cond is None:
            copy.start()
        else:
            pl.when(cond)(copy.start)
        self.sent.append((cond, copy))

    def drain(self):
        for cond, copy in self.sent:
            if cond is None:
                copy.wait_send()
            else:
                pl.when(cond)(copy.wait_send)


def arrived(ref, sem):
    pltpu.make_async_copy(ref, ref, sem).wait()


def split(v):
    hi = v.astype(BF)
    return hi, (v - hi.astype(F32)).astype(BF)


def dot3(a, b, ca, cb):
    dims = (((ca,), (cb,)), ((), ()))

    def one(u, v):
        return lax.dot_general(u, v, dims, preferred_element_type=F32)

    return one(a[0], b[1]) + one(a[1], b[0]) + one(a[0], b[0])


def dot1(a, b):
    return lax.dot_general(a, b, (((1,), (1,)), ((), ())), preferred_element_type=F32)


def row(v, i):
    return jnp.broadcast_to(v[i : i + 1, :], (8, B))


def lane(v, i):
    return jnp.broadcast_to(v[:, i : i + 1], (8, B))


def leaf(tiles, eye, sub):
    out = []
    for m in range(len(tiles)):
        top, unit = tiles[m], eye[m]
        cols = [[lane(tiles[i], 8 * m + b) for b in range(8)] for i in range(m, len(tiles))]
        scale, factors = None, []
        for k in range(8):
            r = lax.rsqrt(row(cols[0][k], k))
            inv = r * r
            scale = r if scale is None else jnp.where(sub == k, r, scale)
            pivots = [row(cols[0][k], b) for b in range(k + 1, 8)]
            f = [v[k] * inv for v in cols]
            for v, g in zip(cols, f):
                for b in range(k + 1, 8):
                    v[b] = v[b] - g * pivots[b - k - 1]
            if k < 7:
                below = jnp.where(sub > k, f[0], 0.0)
                top = top - below * row(top, k)
                unit = unit - below * row(unit, k)
            factors.append(f[1:])
        for n, i in enumerate(range(m + 1, len(tiles))):
            da = functools.reduce(jnp.add, [factors[k][n] * row(top, k) for k in range(8)])
            du = functools.reduce(jnp.add, [factors[k][n] * row(unit, k) for k in range(8)])
            tiles[i] = tiles[i] - da
            eye[i] = eye[i] - du
        out.append((unit * scale, top * scale))
    return out


def fill(dst, base, act, sig_cols, stat):
    a = act.astype(F32)
    for o in range(2):
        v = sig_cols[:, o : o + 1] * a
        v = (v - stat[2 * o : 2 * o + 1]) * stat[2 * o + 1 : 2 * o + 2]
        dst[base : base + ROWS, o * COLS : (o + 1) * COLS] = v.astype(BF)


def cols_of(rows):
    return jnp.transpose(rows)


def greet(s, p):
    c, k = lax.rem(s, 2), s // 2
    barrier = pltpu.get_barrier_semaphore()

    def signal(to_s, to_p):
        pl.semaphore_signal(
            barrier, inc=1, device_id={"samp": to_s, "par": to_p}, device_id_type=MESH
        )

    for i in range(1, NS):
        signal(lax.rem(s + i, NS), p)
    for i in range(1, NP):
        signal(s, lax.rem(p + i, NP))

    @pl.when(k != p)
    def _():
        signal(2 * p + c, k)

    pl.semaphore_wait(barrier, NS + NP - 2 + jnp.where(k == p, 0, 1))


class Place:
    def __init__(self):
        s, p = lax.axis_index("samp"), lax.axis_index("par")
        self.s, self.p = s, p
        self.c, self.k = lax.rem(s, 2), s // 2
        self.x, self.zh = lax.rem(self.k, NX), self.k // NX
        self.y, self.zl = p // NZ, lax.rem(p, NZ)
        self.other = s + 1 - 2 * self.c
        self.up, self.down = lax.rem(self.y + 1, NY), lax.rem(self.y + NY - 1, NY)
        self.far, self.lo = lax.rem(self.y + 2, NY), 1 - self.zl
        self.ahead = jnp.where(self.c == 0, self.up, self.down)
        self.behind = jnp.where(self.c == 0, self.down, self.up)
        self.relay = jnp.logical_or(
            jnp.logical_and(self.x == 1, self.c == 0), jnp.logical_and(self.x == 3, self.c == 1)
        )

    def samp_of(self, zz, xx):
        return 2 * (zz * NX + xx) + self.c

    def tree(self):
        return [
            (self.samp_of(self.zh, 1), self.x == 0),
            (self.samp_of(self.zh, 3), self.x == 0),
            (self.samp_of(1, 0), self.k == 0),
            (self.samp_of(self.zh, 2), self.relay),
        ]


def par_gather(here, net, buf, slot, pieces, sems, own, core, between):
    two_send, two_recv, core_send, core_recv = sems
    s, p, y, zl = here.s, here.p, here.y, here.zl
    up, down, far, lo = here.up, here.down, here.far, here.lo
    step = ROWS // pieces

    def par_of(yy, ll):
        return yy * NZ + ll

    def part(q, t):
        return buf.at[slot, q, pl.ds(t * step, step), :]

    def pass_on(q, t, i, to):
        net.send(part(q, t), part(q, t), two_send.at[i, t], two_recv.at[i, t], s, to)

    def across(q, t, i):
        net.send(part(q, t), part(q, t), core_send.at[i, t], core_recv.at[i, t], here.other, p, core)

    def stage_own(t):
        own(part(p, t), t)
        pass_on(p, t, 1, par_of(up, zl))
        pass_on(p, t, 2, par_of(down, zl))
        pass_on(p, t, 0, par_of(y, lo))
        across(p, t, 0)

    def stage_near(t):
        q = par_of(y, lo)
        arrived(part(q, t), two_recv.at[0, t])
        pass_on(q, t, 3, par_of(up, zl))
        pass_on(q, t, 4, par_of(down, zl))
        across(q, t, 1)
        qu, qd = par_of(down, zl), par_of(up, zl)
        arrived(part(qu, t), two_recv.at[1, t])
        arrived(part(qd, t), two_recv.at[2, t])
        pass_on(par_of(here.behind, zl), t, 5, par_of(here.ahead, zl))
        across(qu, t, 2)
        across(qd, t, 3)

    def stage_far(t):
        q = par_of(far, zl)
        arrived(part(q, t), two_recv.at[5, t])
        pass_on(q, t, 6, par_of(y, lo))
        across(q, t, 4)
        qu, qd = par_of(down, lo), par_of(up, lo)
        arrived(part(qu, t), two_recv.at[3, t])
        arrived(part(qd, t), two_recv.at[4, t])
        across(qu, t, 5)
        across(qd, t, 6)

    def stage_last(t):
        q = par_of(far, lo)
        arrived(part(q, t), two_recv.at[6, t])
        across(q, t, 7)

    for t in range(pieces + 3):
        for lag, stage in enumerate((stage_own, stage_near, stage_far, stage_last)):
            if 0 <= t - lag < pieces:
                stage(t - lag)
        between(t)

    def from_core():
        order = [
            (y, zl), (y, lo), (down, zl), (up, zl), (far, zl), (down, lo), (up, lo), (far, lo),
        ]
        for t in range(pieces):
            for i, (yy, ll) in enumerate(order):
                other = buf.at[1 - here.c, par_of(yy, ll), pl.ds(t * step, step), :]
                arrived(other, core_recv.at[i, t])

    return from_core


def own_sums(act, sig):
    def add(i, sums):
        rows = pl.ds(pl.multiple_of(i * 80, 80), 80)
        a = act[rows, :].astype(F32)
        g = sig[rows, :]
        new = []
        for o in range(2):
            v = g[:, o : o + 1] * a
            new.append(sums[2 * o] + jnp.sum(v.reshape(10, 8, COLS), axis=0))
            new.append(sums[2 * o + 1] + jnp.sum((v * v).reshape(10, 8, COLS), axis=0))
        return tuple(new)

    zero = jnp.zeros((8, COLS), F32)
    sums = lax.fori_loop(0, ROWS // 80, add, (zero,) * 4)
    return jnp.concatenate(
        [jnp.sum(v, axis=0, keepdims=True) for v in sums] + [jnp.zeros((4, COLS), F32)], axis=0
    )


def statistics(total):
    count, width = float(NS * ROWS), float(2 * COLS * NP)
    rows = []
    for o in range(2):
        average = total[2 * o : 2 * o + 1] / count
        second = total[2 * o + 1 : 2 * o + 2] / count
        rows += [average, 1.0 / jnp.sqrt(width * (second - average * average + EPSILON))]
    return jnp.concatenate(rows + [jnp.zeros((4, COLS), F32)], axis=0)


def factor_step(j, uu, diag, sub, ln):
    j0 = pl.multiple_of(j * B, B)
    here = pl.ds(j0, B)
    tiles = [uu[pl.ds(pl.multiple_of(j0 + 8 * i, 8), 8), here] for i in range(B // 8)]
    eye = [jnp.where(ln == sub + 8 * i, 1.0, 0.0).astype(F32) for i in range(B // 8)]
    for i, (w, u) in enumerate(leaf(tiles, eye, sub)):
        rows = pl.ds(pl.multiple_of(j0 + 8 * i, 8), 8)
        uu[rows, here] = w
        diag[rows, :] = u


def mega_kernel(
    act, sig, sig_rows, gram, panel,
    blk, ac, uu, lead, diag, jr, jw, mom, moms, sigs, stat, stats, sig_r, sig_c, sig_0,
    own_sem, a_two_send, a_two_recv, a_core_send, a_core_recv,
    b_two_send, b_two_recv, b_core_send, b_core_recv, one_send, one_recv,
    t_send, t_recv, col_send, col_recv, core_send, core_recv,
    u_send, u_recv, u_core_send, u_core_recv,
    mom_send, mom_recv, sig_send, sig_recv, stat_send, stat_recv,
):
    here = Place()
    s, p, c, k = here.s, here.p, here.c, here.k
    own_slot = jnp.where(k == 0, c, 2)
    net = Copies()
    first = pltpu.make_async_copy(act, blk.at[own_slot, p], own_sem.at[0])
    first.start()
    turn = pltpu.make_async_copy(act, ac.at[c, k], own_sem.at[1])

    @pl.when(k == p)
    def _():
        turn.start()

    greet(s, p)
    first.wait()

    def turn_away(cond):
        net.send(act, ac.at[c, p], t_send, t_recv, 2 * p + c, k, jnp.logical_and(cond, k != p))

    def no_wait(ref, t):
        pass

    def between(t):
        if t == 0:
            for i in range(1, NS):
                net.send(sig_rows, sigs.at[s], sig_send.at[i], sig_recv.at[s], lax.rem(s + i, NS), p)
            mom[...] = own_sums(act, sig)
            for i in range(1, NS):
                net.send(mom, moms.at[s], mom_send.at[i], mom_recv.at[s], lax.rem(s + i, NS), p)
            moms[s] = mom[...]
            sigs[s] = sig_rows[...]
            for i, (to, cond) in enumerate(here.tree()[:3]):
                for n in range(BCH):
                    ref = blk.at[c, p, pl.ds(n * (ROWS // BCH), ROWS // BCH), :]
                    net.send(ref, ref, one_send.at[i, n], one_recv.at[n], to, p, k == 0)
            turn_away(k > 0)
        if t == 1:
            for i in range(1, NS):
                j = lax.rem(s + i, NS)
                arrived(moms.at[j], mom_recv.at[j])
            total = moms[0]
            for j in range(1, NS):
                total = total + moms[j]
            stat[...] = statistics(total)
            for i in range(1, NP):
                net.send(stat, stats.at[p], stat_send.at[i], stat_recv.at[p], s, lax.rem(p + i, NP))
            stats[p] = stat[...]

    from_core = par_gather(
        here, net, blk, own_slot, CH, (a_two_send, a_two_recv, a_core_send, a_core_recv),
        no_wait, k == 0, between,
    )
    turn_away(k == 0)
    for i in range(1, NS):
        j = lax.rem(s + i, NS)
        arrived(sigs.at[j], sig_recv.at[j])
    for i in range(1, NP):
        j = lax.rem(p + i, NP)
        arrived(stats.at[j], stat_recv.at[j])
    sig_r[...] = cols_of(sigs[s])
    for h in range(2):
        sig_c[h] = cols_of(sigs[2 * p + h])
        sig_0[h] = cols_of(sigs[h])

    def columns_out():
        @pl.when(k == p)
        def _():
            turn.wait()

        @pl.when(k != p)
        def _():
            arrived(ac.at[c, k], t_recv)

        copies = []
        for i in range(1, NP):
            to = lax.rem(k + i, NP)
            copies.append(
                far_copy(ac.at[c, k], ac.at[c, k], col_send.at[i], col_recv.at[k], 2 * to + c, p)
            )
        copies.append(far_copy(ac.at[c, k], ac.at[c, k], core_send.at[0], core_recv.at[k], here.other, p))
        return copies

    def columns_across():
        copies = []
        for i in range(1, NP):
            j = lax.rem(k + i, NP)
            copies.append(far_copy(ac.at[c, j], ac.at[c, j], core_send.at[i], core_recv.at[j], here.other, p))
        return copies

    def start_across():
        for i, copy in enumerate(columns_across()):
            j = lax.rem(k + i + 1, NP)
            arrived(ac.at[c, j], col_recv.at[j])
            copy.start()

    def columns_done():
        for j in range(NP):
            arrived(ac.at[1 - c, j], core_recv.at[j])

    def own_gram():
        gram[...] = jnp.zeros_like(gram)

        def add(q, carry):
            fill(jr, 0, blk[own_slot, q], sig_r, stats[q])
            for h in range(2):
                fill(jw, h * ROWS, ac[h, q], sig_c[h], stats[q])
            gram[...] += dot1(jr[...], jw[...])
            return carry

        lax.fori_loop(0, NP, add, 0)
        i = lax.broadcasted_iota(jnp.int32, (ROWS, WIDE), 0) + s * ROWS
        j = lax.broadcasted_iota(jnp.int32, (ROWS, WIDE), 1) + p * WIDE
        gram[...] += jnp.where(i == j, DAMPING, 0.0).astype(F32)

    def u_rows(jj, half):
        return uu.at[pl.ds(jj * B + half * (B // 2), B // 2), jj * B :]

    def u_copies(jj):
        ref = u_rows(jj, c)
        return [
            (far_copy(ref, ref, u_send.at[i, jj], u_recv.at[jj], to, p), cond)
            for i, (to, cond) in enumerate(here.tree())
        ]

    def u_across(jj):
        ref = u_rows(jj, c)
        return far_copy(ref, ref, u_core_send.at[jj], u_core_recv.at[jj], here.other, p)

    @pl.when(k == 0)
    def _():
        from_core()
        uu[...] = jnp.zeros_like(uu)

        def add(q, carry):
            for h in range(2):
                fill(jw, h * ROWS, blk[h, q], sig_0[h], stats[q])
            for r in range(WIDE // COLS):
                rows = slice(r * COLS, (r + 1) * COLS)
                uu[rows, r * COLS :] += dot1(jw[rows, :], jw[r * COLS :, :])
            return carry

        lax.fori_loop(0, NP, add, 0)
        for copy in columns_out():
            copy.start()
        sub = lax.broadcasted_iota(jnp.int32, (8, B), 0)
        ln = lax.broadcasted_iota(jnp.int32, (8, B), 1)
        for r in range(NB):
            rows = slice(r * B, (r + 1) * B)
            i = lax.broadcasted_iota(jnp.int32, (B, B), 0)
            j = lax.broadcasted_iota(jnp.int32, (B, B), 1)
            uu[rows, rows] += jnp.where(i == j, DAMPING, 0.0).astype(F32)

        def body(j, carry):
            factor_step(j, uu, diag, sub, ln)
            for jj in range(NB):

                @pl.when(j == jj)
                def _():
                    rows = slice(jj * B, jj * B + B)
                    low = (jj + 1) * B
                    if jj < NB - 1:
                        x = dot3(split(uu[rows, rows]), split(uu[rows, low:]), 1, 0)
                        uu[rows, low:] = x
                        xs = split(x)
                    for copy, _ in u_copies(jj)[:3]:
                        copy.start()
                    for t in range(jj + 1, NB):
                        at = t * B - low
                        left = (xs[0][:, at : at + B], xs[1][:, at : at + B])
                        right = (xs[0][:, at:], xs[1][:, at:])
                        uu[t * B : t * B + B, t * B :] -= dot3(left, right, 0, 0)
                    if jj == 6:
                        start_across()

            return carry

        lax.fori_loop(0, NB, body, 0)
        columns_done()
        own_gram()
        for jj in range(NB):
            for copy, _ in u_copies(jj)[:3]:
                copy.wait_send()
        for j in range(NB):
            uu[j * B : j * B + B, j * B : j * B + B] = diag[j * B : j * B + B, :]
        width = WIDE // NP
        m = uu[pl.ds(pl.multiple_of(p * width, 8), width), pl.ds(pl.multiple_of(s * ROWS, B), ROWS)]
        i = lax.broadcasted_iota(jnp.int32, (width, ROWS), 0) + p * width
        j = lax.broadcasted_iota(jnp.int32, (width, ROWS), 1) + s * ROWS
        panel[...] = jnp.transpose(jnp.where(i <= j, m, 0.0))

    @pl.when(k > 0)
    def _():
        inner = Copies()
        for copy in columns_out():
            copy.start()

        def own(ref, t):
            arrived(ref, one_recv.at[t])
            for i, (to, cond) in enumerate(here.tree()):
                if i != 2:
                    inner.send(ref, ref, one_send.at[i, t], one_recv.at[t], to, p, cond)

        come = par_gather(
            here, inner, blk, c, BCH, (b_two_send, b_two_recv, b_core_send, b_core_recv),
            own, None, lambda t: None,
        )
        start_across()
        come()
        lead[...] = jnp.zeros_like(lead)

        def add(q, carry):
            fill(jr, 0, blk[2, q], sig_r, stats[q])
            for h in range(2):
                fill(jw, h * ROWS, blk[h, q], sig_0[h], stats[q])
            lead[...] += dot1(jr[...], jw[...])
            return carry

        lax.fori_loop(0, NP, add, 0)
        columns_done()
        own_gram()
        for jj in range(NB):
            arrived(u_rows(jj, c), u_recv.at[jj])
            for i, (copy, cond) in enumerate(u_copies(jj)):
                if i != 2:
                    pl.when(cond)(copy.start)
            u_across(jj).start()
            arrived(u_rows(jj, 1 - c), u_core_recv.at[jj])
            rows = slice(jj * B, jj * B + B)
            done = dot3(split(lead[:, rows]), split(uu[rows, rows]), 1, 1)
            lead[:, rows] = done
            if jj < NB - 1:
                halves = split(done)

                def minus(t, carry):
                    at = pl.ds(pl.multiple_of(t * B, B), B)
                    lead[:, at] -= dot3(halves, split(uu[rows, at]), 1, 0)
                    return carry

                lax.fori_loop(jj + 1, NB, minus, 0)
        width = WIDE // NP
        for pp in range(NP):

            @pl.when(p == pp)
            def _():
                panel[...] = lead[:, pp * width : (pp + 1) * width]

        for jj in range(NB):
            for i, (copy, cond) in enumerate(u_copies(jj)):
                if i != 2:
                    pl.when(cond)(copy.wait_send)
            u_across(jj).wait_send()
        inner.drain()

    for copy in columns_sent(here, ac, col_send, col_recv, core_send, core_recv):
        copy.wait_send()
    net.drain()


def columns_sent(here, ac, col_send, col_recv, core_send, core_recv):
    c, k, p = here.c, here.k, here.p
    copies = []
    for i in range(1, NP):
        to = lax.rem(k + i, NP)
        copies.append(far_copy(ac.at[c, k], ac.at[c, k], col_send.at[i], col_recv.at[k], 2 * to + c, p))
    for i in range(NP):
        j = lax.rem(k + i, NP)
        copies.append(far_copy(ac.at[c, j], ac.at[c, j], core_send.at[i], core_recv.at[j], here.other, p))
    return copies


def far_copy(src, dst, send_sem, recv_sem, s, p):
    return pltpu.make_async_remote_copy(
        src_ref=src,
        dst_ref=dst,
        send_sem=send_sem,
        recv_sem=recv_sem,
        device_id={"samp": s, "par": p},
        device_id_type=MESH,
    )


def per_device(activations, signal):
    sig = signal.astype(F32)
    sig_rows = jnp.pad(sig.T, ((0, 6), (0, 0)))
    dma, vm = pltpu.SemaphoreType.DMA, pltpu.VMEM
    return pl.pallas_call(
        mega_kernel,
        name="gram_and_panels",
        out_shape=(
            jax.ShapeDtypeStruct((ROWS, WIDE), F32),
            jax.ShapeDtypeStruct((ROWS, WIDE // NP), F32),
        ),
        in_specs=[VM, VM, VM],
        out_specs=(VM, VM),
        scratch_shapes=[
            vm((3, NP, ROWS, COLS), BF),
            vm((2, NP, ROWS, COLS), BF),
            vm((WIDE, WIDE), F32),
            vm((ROWS, WIDE), F32),
            vm((WIDE, B), F32),
            vm((ROWS, 2 * COLS), BF),
            vm((WIDE, 2 * COLS), BF),
            vm((8, COLS), F32),
            vm((NS, 8, COLS), F32),
            vm((NS, 8, ROWS), F32),
            vm((8, COLS), F32),
            vm((NP, 8, COLS), F32),
            vm((ROWS, 8), F32),
            vm((2, ROWS, 8), F32),
            vm((2, ROWS, 8), F32),
            dma((2,)),
            dma((7, CH)), dma((7, CH)), dma((8, CH)), dma((8, CH)),
            dma((7, BCH)), dma((7, BCH)), dma((8, BCH)), dma((8, BCH)), dma((4, BCH)), dma((BCH,)),
            dma, dma, dma((NP,)), dma((NP,)), dma((NP,)), dma((NP,)),
            dma((4, NB)), dma((NB,)), dma((NB,)), dma((NB,)),
            dma((NS,)), dma((NS,)), dma((NS,)), dma((NS,)), dma((NP,)), dma((NP,)),
        ],
        compiler_params=pltpu.CompilerParams(
            collective_id=0, has_side_effects=True, vmem_limit_bytes=60 * 2**20
        ),
    )(activations, sig, sig_rows)


def solution(mesh):
    return jax.shard_map(
        per_device,
        mesh=mesh,
        in_specs=(P("samp", "par"), P("samp", None)),
        out_specs=(P("samp", "par"), P("samp", "par")),
        check_vma=False,
    )
```

time: 1370 us -> 200 us (0.15); the launches traced: 1350 us -> 200 us
  waiting for transfers between devices: 859 us -> 0 us
  other arithmetic: 342 us -> 0.69 us
  Pallas kernels: 0 us -> 191 us
  matrix products: 59.1 us -> 0 us
  local copies, waits for them, and re-layouts: 44.9 us -> 8.07 us
  blocking collectives: 27.9 us -> 0 us
  between operations: 21.2 us -> 0.64 us
    psum x5 -> x0, waiting for transfers between devices: 743 us -> none  [from_root(): return lax.psum(jnp.where(mine, value, jnp.zeros_like(value)), axis)]
    another operation x42 -> x0, other arithmetic: 320 us -> none  [the longest x19 108 us: per_device(): jnp.linalg.cholesky(jnp.where(samp_index == 1, update, identity))]
    pallas_call x0 -> x1, Pallas kernels: none -> 191 us  [per_device(): pl.pallas_call(mega_kernel, name='gram_and_panels', out_shape=(jax.ShapeD...]
    all_gather x1 -> x0, waiting for transfers between devices: 116 us -> none  [per_device(): lax.all_gather(local_rows, 'par', axis=2, tiled=True)]
    another operation x34 -> x0, matrix products: 37.2 us -> none  [the longest x18 23.5 us: right_solve(): return jax.scipy.linalg.solve_triangular(factor, block.T, lower=True).T]
    another operation x51 -> x0, local copies, waits for them, and re-layouts: 30.7 us -> none  [the longest x41 29.2 us: right_solve(): return jax.scipy.linalg.solve_triangular(factor, block.T, lower=True).T]
    psum x1 -> x0, blocking collectives: 27.9 us -> none  [per_device(): moment_one, moment_two = lax.psum((sum_one, sum_two), 'samp')]
    dot_general x4 -> x0, matrix products: 21.9 us -> none  [the longest x2 13.1 us: per_device(): lax.dot_general(full_rows, partner, (((1,), (1,)), ((), ())), preferred_e...]
  transfers between devices with their start and end apart: 6 -> 0, of which waited for: 6 -> 0; matrix products, arithmetic and copies ran while one was open for 0% -> 0% of each run, Pallas kernels for 0% -> 0%
where the time goes in v3:
time: 200 us
  Pallas kernels  191 us (96%)
  local copies, waits for them, and re-layouts  8.07 us (4%)
    pallas_call x1, Pallas kernels, per_device(): pl.pallas_call(mega_kernel, name='gram_and_panels', out_shape=(jax.ShapeD...  191 us

profile of v3, /device:TPU:77, one launch (start us, length us, event | category | flops | bytes accessed | tf_op | source)
XLA Modules:
  0.0 200.2 jit_solution(8876172639673274490)
XLA Ops:
  0.6 0.7 convert_bitcast_fusion
  1.3 0.6 pad.4.sig_rows
  1.9 1.6 copy.4.sig
  3.5 190.8 %gram_and_panels.1 = (f32[640,1280]{1,0:T(8,128)}, f32[640,160]{1,0:T(8,128)}) custom-call(bf16[640,256]{1,0:T(8,128)(2,1)} %act.1, f32[640,2]{1,0:T(8,128)} %copy.4.sig, f32[8,640]{1,0:T(8,128)} %pad.4.sig_rows), custom_call_target="tpu_custom_call" | custom-call | tf_op jit(solution)/shard_map/gram_and_panels/pallas_call | solution.py:587
  194.3 2.0 %copy.5 = f32[640,160]{0,1:T(8,128)} copy(f32[640,160]{1,0:T(8,128)} %get-tuple-element.3) | data formatting | bytes 819200 | tf_op jit(solution)/shard_map/gram_and_panels/pallas_call | solution.py:587
  196.3 3.8 %copy.7 = f32[640,1280]{1,0:T(8,128)} copy(f32[640,1280]{1,0:T(8,128)} %get-tuple-element.6) | data formatting | bytes 6553600

commit v4 on v3

--- a/solution.py
+++ b/solution.py
@@ -159,10 +159,6 @@
         self.x, self.zh = lax.rem(self.k, NX), self.k // NX
         self.y, self.zl = p // NZ, lax.rem(p, NZ)
         self.other = s + 1 - 2 * self.c
-        self.up, self.down = lax.rem(self.y + 1, NY), lax.rem(self.y + NY - 1, NY)
-        self.far, self.lo = lax.rem(self.y + 2, NY), 1 - self.zl
-        self.ahead = jnp.where(self.c == 0, self.up, self.down)
-        self.behind = jnp.where(self.c == 0, self.down, self.up)
         self.relay = jnp.logical_or(
             jnp.logical_and(self.x == 1, self.c == 0), jnp.logical_and(self.x == 3, self.c == 1)
         )
@@ -179,76 +175,101 @@
         ]
 
 
-def par_gather(here, net, buf, slot, pieces, sems, own, core, between):
-    two_send, two_recv, core_send, core_recv = sems
-    s, p, y, zl = here.s, here.p, here.y, here.zl
-    up, down, far, lo = here.up, here.down, here.far, here.lo
-    step = ROWS // pieces
-
-    def par_of(yy, ll):
-        return yy * NZ + ll
-
-    def part(q, t):
-        return buf.at[slot, q, pl.ds(t * step, step), :]
-
-    def pass_on(q, t, i, to):
-        net.send(part(q, t), part(q, t), two_send.at[i, t], two_recv.at[i, t], s, to)
-
-    def across(q, t, i):
-        net.send(part(q, t), part(q, t), core_send.at[i, t], core_recv.at[i, t], here.other, p, core)
-
-    def stage_own(t):
-        own(part(p, t), t)
-        pass_on(p, t, 1, par_of(up, zl))
-        pass_on(p, t, 2, par_of(down, zl))
-        pass_on(p, t, 0, par_of(y, lo))
-        across(p, t, 0)
-
-    def stage_near(t):
-        q = par_of(y, lo)
-        arrived(part(q, t), two_recv.at[0, t])
-        pass_on(q, t, 3, par_of(up, zl))
-        pass_on(q, t, 4, par_of(down, zl))
-        across(q, t, 1)
-        qu, qd = par_of(down, zl), par_of(up, zl)
-        arrived(part(qu, t), two_recv.at[1, t])
-        arrived(part(qd, t), two_recv.at[2, t])
-        pass_on(par_of(here.behind, zl), t, 5, par_of(here.ahead, zl))
-        across(qu, t, 2)
-        across(qd, t, 3)
-
-    def stage_far(t):
-        q = par_of(far, zl)
-        arrived(part(q, t), two_recv.at[5, t])
-        pass_on(q, t, 6, par_of(y, lo))
-        across(q, t, 4)
-        qu, qd = par_of(down, lo), par_of(up, lo)
-        arrived(part(qu, t), two_recv.at[3, t])
-        arrived(part(qd, t), two_recv.at[4, t])
-        across(qu, t, 5)
-        across(qd, t, 6)
-
-    def stage_last(t):
-        q = par_of(far, lo)
-        arrived(part(q, t), two_recv.at[6, t])
-        across(q, t, 7)
-
-    for t in range(pieces + 3):
-        for lag, stage in enumerate((stage_own, stage_near, stage_far, stage_last)):
-            if 0 <= t - lag < pieces:
-                stage(t - lag)
-        between(t)
-
-    def from_core():
-        order = [
-            (y, zl), (y, lo), (down, zl), (up, zl), (far, zl), (down, lo), (up, lo), (far, lo),
-        ]
-        for t in range(pieces):
-            for i, (yy, ll) in enumerate(order):
-                other = buf.at[1 - here.c, par_of(yy, ll), pl.ds(t * step, step), :]
-                arrived(other, core_recv.at[i, t])
-
-    return from_core
+class Gather:
+    def __init__(self, here, buf, index, ring, pair, where, pieces, sems, core=True, by_ring=False):
+        self.here, self.buf, self.index = here, buf, index
+        self.ring, self.pair, self.where = ring, pair, where
+        self.up, self.down = lax.rem(ring + 1, 4), lax.rem(ring + 3, 4)
+        self.far, self.lo = lax.rem(ring + 2, 4), 1 - pair
+        self.ahead = jnp.where(here.c == 0, self.up, self.down)
+        self.behind = jnp.where(here.c == 0, self.down, self.up)
+        self.pieces, self.step, self.sems = pieces, ROWS // pieces, sems
+        self.core, self.by_ring = core, by_ring
+
+    def part(self, r, q, t, other=False):
+        slot, _, _ = self.where(r, q)
+        index = 1 - self.index if other else self.index
+        return self.buf.at[index, slot, pl.ds(t * self.step, self.step), :]
+
+    def wait(self, r, q, t, i):
+        return ("wait", self.part(r, q, t), self.sems[1].at[i, t])
+
+    def send(self, r, q, t, i, to_r, to_q):
+        _, to_s, to_p = self.where(to_r, to_q)
+        ref = self.part(r, q, t)
+        copy = far_copy(ref, ref, self.sems[0].at[i, t], self.sems[1].at[i, t], to_s, to_p)
+        return ("send", copy, None)
+
+    def across(self, r, q, t, i):
+        ref, here = self.part(r, q, t), self.here
+        copy = far_copy(ref, ref, self.sems[2].at[i, t], self.sems[3].at[i, t], here.other, here.p)
+        return ("send", copy, None if self.core is True else self.core)
+
+    def events(self, stage, t):
+        r, q, up, down, far, lo = self.ring, self.pair, self.up, self.down, self.far, self.lo
+        if stage == 0:
+            return [
+                self.send(r, q, t, 1, up, q),
+                self.send(r, q, t, 2, down, q),
+                self.send(r, q, t, 0, r, lo),
+                self.across(r, q, t, 0),
+            ]
+        if stage == 1:
+            return [
+                self.wait(r, lo, t, 0),
+                self.send(r, lo, t, 3, up, q),
+                self.send(r, lo, t, 4, down, q),
+                self.across(r, lo, t, 1),
+                self.wait(down, q, t, 1),
+                self.wait(up, q, t, 2),
+                self.send(self.behind, q, t, 5, self.ahead, q),
+                self.across(down, q, t, 2),
+                self.across(up, q, t, 3),
+            ]
+        if stage == 2:
+            hand_on = [self.send(far, q, t, 6, r, lo)]
+            relayed = [self.send(self.behind, lo, t, 6, self.ahead, q)]
+            return [
+                self.wait(far, q, t, 5),
+                *([] if self.by_ring else hand_on),
+                self.across(far, q, t, 4),
+                self.wait(down, lo, t, 3),
+                self.wait(up, lo, t, 4),
+                *(relayed if self.by_ring else []),
+                self.across(down, lo, t, 5),
+                self.across(up, lo, t, 6),
+            ]
+        return [self.wait(far, lo, t, 6), self.across(far, lo, t, 7)]
+
+    def run(self, stage, t):
+        for event in self.events(stage, t):
+            if event[0] == "wait":
+                arrived(*event[1:])
+            elif event[2] is None:
+                event[1].start()
+            else:
+                pl.when(event[2])(event[1].start)
+
+    def run_all(self, stage):
+        for t in range(self.pieces):
+            self.run(stage, t)
+
+    def from_core(self):
+        r, q, up, down, far, lo = self.ring, self.pair, self.up, self.down, self.far, self.lo
+        order = [(r, q), (r, lo), (down, q), (up, q), (far, q), (down, lo), (up, lo), (far, lo)]
+        for t in range(self.pieces):
+            for i, (a, b) in enumerate(order):
+                arrived(self.part(a, b, t, other=True), self.sems[3].at[i, t])
+
+    def drain(self):
+        for stage in range(4):
+            for t in range(self.pieces):
+                for kind, copy, cond in self.events(stage, t):
+                    if kind == "send":
+                        if cond is None:
+                            copy.wait_send()
+                        else:
+                            pl.when(cond)(copy.wait_send)
 
 
 def own_sums(act, sig):
@@ -292,12 +313,12 @@
 
 
 def mega_kernel(
-    act, sig, sig_rows, gram, panel,
-    blk, ac, uu, lead, diag, jr, jw, mom, moms, sigs, stat, stats, sig_r, sig_c, sig_0,
+    act, sig, gram, panel,
+    blk, ac, uu, lead, diag, jr, jw, mom, moms, sigs, stat, stats, sig_own, sig_r, sig_c, sig_0,
     own_sem, a_two_send, a_two_recv, a_core_send, a_core_recv,
-    b_two_send, b_two_recv, b_core_send, b_core_recv, one_send, one_recv,
-    t_send, t_recv, col_send, col_recv, core_send, core_recv,
-    u_send, u_recv, u_core_send, u_core_recv,
+    b_two_send, b_two_recv, b_core_send, b_core_recv,
+    c_two_send, c_two_recv, c_core_send, c_core_recv, one_send, one_recv,
+    t_send, t_recv, u_send, u_recv, u_core_send, u_core_recv,
     mom_send, mom_recv, sig_send, sig_recv, stat_send, stat_recv,
 ):
     here = Place()
@@ -312,30 +333,61 @@
     def _():
         turn.start()
 
+    sig_own[...] = jnp.concatenate([sig[...].astype(F32), jnp.zeros((6, ROWS), F32)], axis=0)
+    sigs[s] = sig_own[...]
+    sig_r[...] = cols_of(sig_own[...])
     greet(s, p)
     first.wait()
 
+    def on_par(r, q):
+        return r * NZ + q, s, r * NZ + q
+
+    def on_samp(r, q):
+        return q * NX + r, here.samp_of(q, r), p
+
+    rows_in = Gather(
+        here, blk, own_slot, here.y, here.zl, on_par, CH,
+        (a_two_send, a_two_recv, a_core_send, a_core_recv), core=k == 0,
+    )
+    lead_in = Gather(
+        here, blk, c, here.y, here.zl, on_par, BCH,
+        (b_two_send, b_two_recv, b_core_send, b_core_recv),
+    )
+    cols_in = Gather(
+        here, ac, c, here.x, here.zh, on_samp, BCH,
+        (c_two_send, c_two_recv, c_core_send, c_core_recv), by_ring=True,
+    )
+
     def turn_away(cond):
         net.send(act, ac.at[c, p], t_send, t_recv, 2 * p + c, k, jnp.logical_and(cond, k != p))
 
-    def no_wait(ref, t):
-        pass
-
-    def between(t):
+    def turned():
+        @pl.when(k == p)
+        def _():
+            turn.wait()
+
+        @pl.when(k != p)
+        def _():
+            arrived(ac.at[c, k], t_recv)
+
+    for t in range(CH + 3):
+        for stage in range(4):
+            if 0 <= t - stage < CH:
+                rows_in.run(stage, t - stage)
         if t == 0:
-            for i in range(1, NS):
-                net.send(sig_rows, sigs.at[s], sig_send.at[i], sig_recv.at[s], lax.rem(s + i, NS), p)
-            mom[...] = own_sums(act, sig)
+            for i, (to, cond) in enumerate(here.tree()[:3]):
+                for n in range(BCH):
+                    ref = lead_in.part(here.y, here.zl, n)
+                    net.send(ref, ref, one_send.at[i, n], one_recv.at[n], to, p, k == 0)
+            mom[...] = own_sums(act, sig_r)
             for i in range(1, NS):
                 net.send(mom, moms.at[s], mom_send.at[i], mom_recv.at[s], lax.rem(s + i, NS), p)
             moms[s] = mom[...]
-            sigs[s] = sig_rows[...]
-            for i, (to, cond) in enumerate(here.tree()[:3]):
-                for n in range(BCH):
-                    ref = blk.at[c, p, pl.ds(n * (ROWS // BCH), ROWS // BCH), :]
-                    net.send(ref, ref, one_send.at[i, n], one_recv.at[n], to, p, k == 0)
+        if t == 1:
+            for i in range(1, NS):
+                net.send(sig_own, sigs.at[s], sig_send.at[i], sig_recv.at[s], lax.rem(s + i, NS), p)
             turn_away(k > 0)
-        if t == 1:
+        if t == 3:
             for i in range(1, NS):
                 j = lax.rem(s + i, NS)
                 arrived(moms.at[j], mom_recv.at[j])
@@ -347,60 +399,18 @@
                 net.send(stat, stats.at[p], stat_send.at[i], stat_recv.at[p], s, lax.rem(p + i, NP))
             stats[p] = stat[...]
 
-    from_core = par_gather(
-        here, net, blk, own_slot, CH, (a_two_send, a_two_recv, a_core_send, a_core_recv),
-        no_wait, k == 0, between,
-    )
     turn_away(k == 0)
     for i in range(1, NS):
         j = lax.rem(s + i, NS)
         arrived(sigs.at[j], sig_recv.at[j])
+    for h in range(2):
+        sig_c[h] = cols_of(sigs[2 * p + h])
+        sig_0[h] = cols_of(sigs[h])
     for i in range(1, NP):
         j = lax.rem(p + i, NP)
         arrived(stats.at[j], stat_recv.at[j])
-    sig_r[...] = cols_of(sigs[s])
-    for h in range(2):
-        sig_c[h] = cols_of(sigs[2 * p + h])
-        sig_0[h] = cols_of(sigs[h])
-
-    def columns_out():
-        @pl.when(k == p)
-        def _():
-            turn.wait()
-
-        @pl.when(k != p)
-        def _():
-            arrived(ac.at[c, k], t_recv)
-
-        copies = []
-        for i in range(1, NP):
-            to = lax.rem(k + i, NP)
-            copies.append(
-                far_copy(ac.at[c, k], ac.at[c, k], col_send.at[i], col_recv.at[k], 2 * to + c, p)
-            )
-        copies.append(far_copy(ac.at[c, k], ac.at[c, k], core_send.at[0], core_recv.at[k], here.other, p))
-        return copies
-
-    def columns_across():
-        copies = []
-        for i in range(1, NP):
-            j = lax.rem(k + i, NP)
-            copies.append(far_copy(ac.at[c, j], ac.at[c, j], core_send.at[i], core_recv.at[j], here.other, p))
-        return copies
-
-    def start_across():
-        for i, copy in enumerate(columns_across()):
-            j = lax.rem(k + i + 1, NP)
-            arrived(ac.at[c, j], col_recv.at[j])
-            copy.start()
-
-    def columns_done():
-        for j in range(NP):
-            arrived(ac.at[1 - c, j], core_recv.at[j])
-
-    def own_gram():
-        gram[...] = jnp.zeros_like(gram)
-
+
+    def gram_part(start, stop):
         def add(q, carry):
             fill(jr, 0, blk[own_slot, q], sig_r, stats[q])
             for h in range(2):
@@ -408,10 +418,12 @@
             gram[...] += dot1(jr[...], jw[...])
             return carry
 
-        lax.fori_loop(0, NP, add, 0)
+        lax.fori_loop(start, stop, add, 0)
+
+    def gram_first():
         i = lax.broadcasted_iota(jnp.int32, (ROWS, WIDE), 0) + s * ROWS
         j = lax.broadcasted_iota(jnp.int32, (ROWS, WIDE), 1) + p * WIDE
-        gram[...] += jnp.where(i == j, DAMPING, 0.0).astype(F32)
+        gram[...] = jnp.where(i == j, DAMPING, 0.0).astype(F32)
 
     def u_rows(jj, half):
         return uu.at[pl.ds(jj * B + half * (B // 2), B // 2), jj * B :]
@@ -427,9 +439,12 @@
         ref = u_rows(jj, c)
         return far_copy(ref, ref, u_core_send.at[jj], u_core_recv.at[jj], here.other, p)
 
+    width = WIDE // NP
+    own_cols = pl.ds(pl.multiple_of(p * width, 8), width)
+
     @pl.when(k == 0)
     def _():
-        from_core()
+        rows_in.from_core()
         uu[...] = jnp.zeros_like(uu)
 
         def add(q, carry):
@@ -441,8 +456,8 @@
             return carry
 
         lax.fori_loop(0, NP, add, 0)
-        for copy in columns_out():
-            copy.start()
+        turned()
+        cols_in.run_all(0)
         sub = lax.broadcasted_iota(jnp.int32, (8, B), 0)
         ln = lax.broadcasted_iota(jnp.int32, (8, B), 1)
         for r in range(NB):
@@ -470,56 +485,62 @@
                         left = (xs[0][:, at : at + B], xs[1][:, at : at + B])
                         right = (xs[0][:, at:], xs[1][:, at:])
                         uu[t * B : t * B + B, t * B :] -= dot3(left, right, 0, 0)
-                    if jj == 6:
-                        start_across()
+                    if jj in (1, 3, 5):
+                        cols_in.run_all((jj + 1) // 2)
 
             return carry
 
         lax.fori_loop(0, NB, body, 0)
-        columns_done()
-        own_gram()
+        cols_in.from_core()
+        gram_first()
+        gram_part(0, NP)
         for jj in range(NB):
             for copy, _ in u_copies(jj)[:3]:
                 copy.wait_send()
         for j in range(NB):
             uu[j * B : j * B + B, j * B : j * B + B] = diag[j * B : j * B + B, :]
-        width = WIDE // NP
-        m = uu[pl.ds(pl.multiple_of(p * width, 8), width), pl.ds(pl.multiple_of(s * ROWS, B), ROWS)]
+        m = uu[own_cols, pl.ds(pl.multiple_of(s * ROWS, B), ROWS)]
         i = lax.broadcasted_iota(jnp.int32, (width, ROWS), 0) + p * width
         j = lax.broadcasted_iota(jnp.int32, (width, ROWS), 1) + s * ROWS
-        panel[...] = jnp.transpose(jnp.where(i <= j, m, 0.0))
+        panel[...] = jnp.where(i <= j, m, 0.0)
 
     @pl.when(k > 0)
     def _():
         inner = Copies()
-        for copy in columns_out():
-            copy.start()
-
-        def own(ref, t):
-            arrived(ref, one_recv.at[t])
-            for i, (to, cond) in enumerate(here.tree()):
-                if i != 2:
-                    inner.send(ref, ref, one_send.at[i, t], one_recv.at[t], to, p, cond)
-
-        come = par_gather(
-            here, inner, blk, c, BCH, (b_two_send, b_two_recv, b_core_send, b_core_recv),
-            own, None, lambda t: None,
-        )
-        start_across()
-        come()
+        for t in range(BCH + 3):
+            if t < BCH:
+                ref = lead_in.part(here.y, here.zl, t)
+                arrived(ref, one_recv.at[t])
+                for i, (to, cond) in enumerate(here.tree()):
+                    if i != 2:
+                        inner.send(ref, ref, one_send.at[i, t], one_recv.at[t], to, p, cond)
+            for stage in range(4):
+                if 0 <= t - stage < BCH:
+                    lead_in.run(stage, t - stage)
+            if t == 1:
+                turned()
+                cols_in.run_all(0)
+        lead_in.from_core()
         lead[...] = jnp.zeros_like(lead)
 
         def add(q, carry):
             fill(jr, 0, blk[2, q], sig_r, stats[q])
             for h in range(2):
                 fill(jw, h * ROWS, blk[h, q], sig_0[h], stats[q])
-            lead[...] += dot1(jr[...], jw[...])
+            lead[...] += dot1(jw[...], jr[...])
             return carry
 
-        lax.fori_loop(0, NP, add, 0)
-        columns_done()
-        own_gram()
+        cols_in.run_all(1)
+        lax.fori_loop(0, NP // 2, add, 0)
+        cols_in.run_all(2)
+        lax.fori_loop(NP // 2, NP, add, 0)
+        cols_in.run_all(3)
+        gram_first()
         for jj in range(NB):
+            if jj in (3, 6):
+                if jj == 3:
+                    cols_in.from_core()
+                gram_part(0 if jj == 3 else NP // 2, NP // 2 if jj == 3 else NP)
             arrived(u_rows(jj, c), u_recv.at[jj])
             for i, (copy, cond) in enumerate(u_copies(jj)):
                 if i != 2:
@@ -527,46 +548,29 @@
             u_across(jj).start()
             arrived(u_rows(jj, 1 - c), u_core_recv.at[jj])
             rows = slice(jj * B, jj * B + B)
-            done = dot3(split(lead[:, rows]), split(uu[rows, rows]), 1, 1)
-            lead[:, rows] = done
+            done = dot3(split(uu[rows, rows]), split(lead[rows, :]), 1, 0)
+            lead[rows, :] = done
             if jj < NB - 1:
                 halves = split(done)
 
                 def minus(t, carry):
                     at = pl.ds(pl.multiple_of(t * B, B), B)
-                    lead[:, at] -= dot3(halves, split(uu[rows, at]), 1, 0)
+                    lead[at, :] -= dot3(split(uu[rows, at]), halves, 0, 0)
                     return carry
 
                 lax.fori_loop(jj + 1, NB, minus, 0)
-        width = WIDE // NP
-        for pp in range(NP):
-
-            @pl.when(p == pp)
-            def _():
-                panel[...] = lead[:, pp * width : (pp + 1) * width]
-
+        panel[...] = lead[own_cols, :]
         for jj in range(NB):
             for i, (copy, cond) in enumerate(u_copies(jj)):
                 if i != 2:
                     pl.when(cond)(copy.wait_send)
             u_across(jj).wait_send()
+        lead_in.drain()
         inner.drain()
 
-    for copy in columns_sent(here, ac, col_send, col_recv, core_send, core_recv):
-        copy.wait_send()
+    cols_in.drain()
+    rows_in.drain()
     net.drain()
-
-
-def columns_sent(here, ac, col_send, col_recv, core_send, core_recv):
-    c, k, p = here.c, here.k, here.p
-    copies = []
-    for i in range(1, NP):
-        to = lax.rem(k + i, NP)
-        copies.append(far_copy(ac.at[c, k], ac.at[c, k], col_send.at[i], col_recv.at[k], 2 * to + c, p))
-    for i in range(NP):
-        j = lax.rem(k + i, NP)
-        copies.append(far_copy(ac.at[c, j], ac.at[c, j], core_send.at[i], core_recv.at[j], here.other, p))
-    return copies
 
 
 def far_copy(src, dst, send_sem, recv_sem, s, p):
@@ -581,23 +585,25 @@
 
 
 def per_device(activations, signal):
-    sig = signal.astype(F32)
-    sig_rows = jnp.pad(sig.T, ((0, 6), (0, 0)))
     dma, vm = pltpu.SemaphoreType.DMA, pltpu.VMEM
-    return pl.pallas_call(
+
+    def gather_sems(pieces):
+        return [dma((7, pieces)), dma((7, pieces)), dma((8, pieces)), dma((8, pieces))]
+
+    gram, panel = pl.pallas_call(
         mega_kernel,
         name="gram_and_panels",
         out_shape=(
             jax.ShapeDtypeStruct((ROWS, WIDE), F32),
-            jax.ShapeDtypeStruct((ROWS, WIDE // NP), F32),
+            jax.ShapeDtypeStruct((WIDE // NP, ROWS), F32),
         ),
-        in_specs=[VM, VM, VM],
+        in_specs=[VM, VM],
         out_specs=(VM, VM),
         scratch_shapes=[
             vm((3, NP, ROWS, COLS), BF),
             vm((2, NP, ROWS, COLS), BF),
             vm((WIDE, WIDE), F32),
-            vm((ROWS, WIDE), F32),
+            vm((WIDE, ROWS), F32),
             vm((WIDE, B), F32),
             vm((ROWS, 2 * COLS), BF),
             vm((WIDE, 2 * COLS), BF),
@@ -606,20 +612,21 @@
             vm((NS, 8, ROWS), F32),
             vm((8, COLS), F32),
             vm((NP, 8, COLS), F32),
+            vm((8, ROWS), F32),
             vm((ROWS, 8), F32),
             vm((2, ROWS, 8), F32),
             vm((2, ROWS, 8), F32),
             dma((2,)),
-            dma((7, CH)), dma((7, CH)), dma((8, CH)), dma((8, CH)),
-            dma((7, BCH)), dma((7, BCH)), dma((8, BCH)), dma((8, BCH)), dma((4, BCH)), dma((BCH,)),
-            dma, dma, dma((NP,)), dma((NP,)), dma((NP,)), dma((NP,)),
+            *gather_sems(CH), *gather_sems(BCH), *gather_sems(BCH),
+            dma((4, BCH)), dma((BCH,)), dma, dma,
             dma((4, NB)), dma((NB,)), dma((NB,)), dma((NB,)),
             dma((NS,)), dma((NS,)), dma((NS,)), dma((NS,)), dma((NP,)), dma((NP,)),
         ],
         compiler_params=pltpu.CompilerParams(
             collective_id=0, has_side_effects=True, vmem_limit_bytes=60 * 2**20
         ),
-    )(activations, sig, sig_rows)
+    )(activations, signal.T)
+    return gram, panel.T
 
 
 def solution(mesh):

time: 200 us -> 178 us (0.89)
  the two profiles are of different devices: /device:TPU:77 before, /device:TPU:21 now
where the time goes in v4:
time: 178 us
  Pallas kernels  172 us (97%)
  local copies, waits for them, and re-layouts  4.65 us (3%)
    pallas_call x1, Pallas kernels, per_device(): pl.pallas_call(mega_kernel, name='gram_and_panels', out_shape=(jax.ShapeD...  172 us
    unnamed x4, local copies, waits for them, and re-layouts  4.65 us

profile of v4, /device:TPU:21, one launch (start us, length us, event | category | flops | bytes accessed | tf_op | source)
XLA Modules:
  0.0 177.8 jit_solution(8384671891433248848)
XLA Ops:
  0.6 172.5 %gram_and_panels.1 = (f32[640,1280]{1,0:T(8,128)}, f32[160,640]{1,0:T(8,128)}) custom-call(bf16[640,256]{1,0:T(8,128)(2,1)} %act.1, bf16[2,640]{1,0:T(2,128)(2,1)} %bitcast.3), custom_call_target="tpu_custom_call" | custom-call | tf_op jit(solution)/shard_map/gram_and_panels/pallas_call | solution.py:593
  173.1 0.0 copy-start
  173.1 3.9 %copy.6 = f32[640,1280]{1,0:T(8,128)} copy(f32[640,1280]{1,0:T(8,128)} %get-tuple-element.8) | data formatting | bytes 6553600
  177.0 0.0 copy-done
  177.0 0.8 copy.7
Async XLA Ops:
  173.1 3.9 %copy-start = (f32[160,640]{1,0:T(8,128)S(1)}, f32[160,640]{1,0:T(8,128)}, u32[]{:S(2)}) copy-start(f32[160,640]{1,0:T(8,128)} %get-tuple-element.5) | copy-start | bytes 1228804

commit v5 on v4

--- a/solution.py
+++ b/solution.py
@@ -127,7 +127,7 @@
 
 
 def cols_of(rows):
-    return jnp.transpose(rows)
+    return jnp.transpose(jnp.concatenate([rows.astype(F32), jnp.zeros((6, ROWS), F32)], axis=0))
 
 
 def greet(s, p):
@@ -159,24 +159,29 @@
         self.x, self.zh = lax.rem(self.k, NX), self.k // NX
         self.y, self.zl = p // NZ, lax.rem(p, NZ)
         self.other = s + 1 - 2 * self.c
-        self.relay = jnp.logical_or(
-            jnp.logical_and(self.x == 1, self.c == 0), jnp.logical_and(self.x == 3, self.c == 1)
-        )
-
     def samp_of(self, zz, xx):
         return 2 * (zz * NX + xx) + self.c
 
     def tree(self):
+        x, zh, c = self.x, self.zh, self.c
+        root = jnp.where(zh == 0, 0, c)
+        turn = lax.rem(x - root + NX, NX)
+        side = jnp.where(c == 0, turn == 1, turn == 3)
         return [
-            (self.samp_of(self.zh, 1), self.x == 0),
-            (self.samp_of(self.zh, 3), self.x == 0),
-            (self.samp_of(1, 0), self.k == 0),
-            (self.samp_of(self.zh, 2), self.relay),
+            (self.samp_of(zh, lax.rem(root + 1, NX)), turn == 0),
+            (self.samp_of(zh, lax.rem(root + 3, NX)), turn == 0),
+            (self.samp_of(1, x), jnp.logical_and(zh == 0, x == c)),
+            (self.samp_of(zh, lax.rem(root + 2, NX)), side),
         ]
 
+    def level(self):
+        root = jnp.where(self.zh == 0, 0, self.c)
+        turn = lax.rem(self.x - root + NX, NX)
+        return jnp.where(self.zh == 0, 0, 1 + self.c) + jnp.where(turn == 2, 2, jnp.where(turn == 0, 0, 1))
+
 
 class Gather:
-    def __init__(self, here, buf, index, ring, pair, where, pieces, sems, core=True, by_ring=False):
+    def __init__(self, here, buf, index, ring, pair, where, pieces, sems, core=True, by_ring=False, busy=None):
         self.here, self.buf, self.index = here, buf, index
         self.ring, self.pair, self.where = ring, pair, where
         self.up, self.down = lax.rem(ring + 1, 4), lax.rem(ring + 3, 4)
@@ -184,7 +189,7 @@
         self.ahead = jnp.where(here.c == 0, self.up, self.down)
         self.behind = jnp.where(here.c == 0, self.down, self.up)
         self.pieces, self.step, self.sems = pieces, ROWS // pieces, sems
-        self.core, self.by_ring = core, by_ring
+        self.core, self.by_ring, self.busy = core, by_ring, busy
 
     def part(self, r, q, t, other=False):
         slot, _, _ = self.where(r, q)
@@ -199,6 +204,29 @@
         ref = self.part(r, q, t)
         copy = far_copy(ref, ref, self.sems[0].at[i, t], self.sems[1].at[i, t], to_s, to_p)
         return ("send", copy, None)
+
+    def relay(self, *args):
+        kind, copy, _ = self.send(*args)
+        return (kind, copy, None if self.busy is None else jnp.logical_not(self.busy))
+
+    def direct(self, t):
+        if self.busy is None:
+            return []
+        r, q, c = self.ring, self.pair, self.here.c
+        end = jnp.where(r == 3, 1, 3)
+        side = jnp.where(c == 0, r == 3, r == 1)
+        ref = self.part(r, q, t)
+        found = []
+        for n, (i, to, cond) in enumerate((
+            (3, 1, jnp.logical_and(r == 0, q == 1)),
+            (4, 3, jnp.logical_and(r == 0, q == 1)),
+            (5, end, jnp.logical_and(side, q == 0)),
+            (6, end, jnp.logical_and(side, q == 1)),
+        )):
+            _, to_s, to_p = self.where(to, 0)
+            copy = far_copy(ref, ref, self.sems[0].at[7 + n, t], self.sems[1].at[i, t], to_s, to_p)
+            found.append(("send", copy, cond))
+        return found
 
     def across(self, r, q, t, i):
         ref, here = self.part(r, q, t), self.here
@@ -213,22 +241,23 @@
                 self.send(r, q, t, 2, down, q),
                 self.send(r, q, t, 0, r, lo),
                 self.across(r, q, t, 0),
+                *self.direct(t),
             ]
         if stage == 1:
             return [
                 self.wait(r, lo, t, 0),
-                self.send(r, lo, t, 3, up, q),
-                self.send(r, lo, t, 4, down, q),
+                self.relay(r, lo, t, 3, up, q),
+                self.relay(r, lo, t, 4, down, q),
                 self.across(r, lo, t, 1),
                 self.wait(down, q, t, 1),
                 self.wait(up, q, t, 2),
-                self.send(self.behind, q, t, 5, self.ahead, q),
+                self.relay(self.behind, q, t, 5, self.ahead, q),
                 self.across(down, q, t, 2),
                 self.across(up, q, t, 3),
             ]
         if stage == 2:
-            hand_on = [self.send(far, q, t, 6, r, lo)]
-            relayed = [self.send(self.behind, lo, t, 6, self.ahead, q)]
+            hand_on = [self.relay(far, q, t, 6, r, lo)]
+            relayed = [self.relay(self.behind, lo, t, 6, self.ahead, q)]
             return [
                 self.wait(far, q, t, 5),
                 *([] if self.by_ring else hand_on),
@@ -314,7 +343,7 @@
 
 def mega_kernel(
     act, sig, gram, panel,
-    blk, ac, uu, lead, diag, jr, jw, mom, moms, sigs, stat, stats, sig_own, sig_r, sig_c, sig_0,
+    blk, ac, uu, lead, diag, jr, jw, mom, moms, sigs, stat, stats, sig_r, sig_c, sig_0,
     own_sem, a_two_send, a_two_recv, a_core_send, a_core_recv,
     b_two_send, b_two_recv, b_core_send, b_core_recv,
     c_two_send, c_two_recv, c_core_send, c_core_recv, one_send, one_recv,
@@ -333,9 +362,8 @@
     def _():
         turn.start()
 
-    sig_own[...] = jnp.concatenate([sig[...].astype(F32), jnp.zeros((6, ROWS), F32)], axis=0)
-    sigs[s] = sig_own[...]
-    sig_r[...] = cols_of(sig_own[...])
+    sigs[s] = sig[...]
+    sig_r[...] = cols_of(sig[...])
     greet(s, p)
     first.wait()
 
@@ -355,7 +383,7 @@
     )
     cols_in = Gather(
         here, ac, c, here.x, here.zh, on_samp, BCH,
-        (c_two_send, c_two_recv, c_core_send, c_core_recv), by_ring=True,
+        (c_two_send, c_two_recv, c_core_send, c_core_recv), by_ring=True, busy=k == 0,
     )
 
     def turn_away(cond):
@@ -369,23 +397,33 @@
         @pl.when(k != p)
         def _():
             arrived(ac.at[c, k], t_recv)
+
+    level = here.level()
+
+    def set_out(copies, when, only):
+        for n in range(BCH) if only is None else [only]:
+            ref = lead_in.part(here.y, here.zl, n)
+            for i, (to, cond) in enumerate(here.tree()):
+                copies.send(ref, ref, one_send.at[i, n], one_recv.at[n], to, p, jnp.logical_and(when, cond))
+
+    def set_in(n):
+        arrived(lead_in.part(here.y, here.zl, n), one_recv.at[n])
 
     for t in range(CH + 3):
         for stage in range(4):
             if 0 <= t - stage < CH:
                 rows_in.run(stage, t - stage)
         if t == 0:
-            for i, (to, cond) in enumerate(here.tree()[:3]):
-                for n in range(BCH):
-                    ref = lead_in.part(here.y, here.zl, n)
-                    net.send(ref, ref, one_send.at[i, n], one_recv.at[n], to, p, k == 0)
+            set_out(net, k == 0, None)
+            wanted = jnp.logical_or(k == 0, k == p)
+            for i in range(1, NS):
+                to = lax.rem(s + i, NS)
+                net.send(sig, sigs.at[s], sig_send.at[i], sig_recv.at[s], to, p, wanted)
             mom[...] = own_sums(act, sig_r)
             for i in range(1, NS):
                 net.send(mom, moms.at[s], mom_send.at[i], mom_recv.at[s], lax.rem(s + i, NS), p)
             moms[s] = mom[...]
         if t == 1:
-            for i in range(1, NS):
-                net.send(sig_own, sigs.at[s], sig_send.at[i], sig_recv.at[s], lax.rem(s + i, NS), p)
             turn_away(k > 0)
         if t == 3:
             for i in range(1, NS):
@@ -400,9 +438,16 @@
             stats[p] = stat[...]
 
     turn_away(k == 0)
-    for i in range(1, NS):
-        j = lax.rem(s + i, NS)
-        arrived(sigs.at[j], sig_recv.at[j])
+
+    @pl.when(level == 1)
+    def _():
+        for n in range(BCH):
+            set_in(n)
+
+    set_out(net, level == 1, None)
+    for h in range(2):
+        for j, cond in ((h, s != h), (2 * p + h, jnp.logical_and(p > 0, s != 2 * p + h))):
+            pl.when(cond)(functools.partial(arrived, sigs.at[j], sig_recv.at[j]))
     for h in range(2):
         sig_c[h] = cols_of(sigs[2 * p + h])
         sig_0[h] = cols_of(sigs[h])
@@ -478,25 +523,25 @@
                         x = dot3(split(uu[rows, rows]), split(uu[rows, low:]), 1, 0)
                         uu[rows, low:] = x
                         xs = split(x)
-                    for copy, _ in u_copies(jj)[:3]:
-                        copy.start()
+                    for copy, cond in u_copies(jj):
+                        pl.when(cond)(copy.start)
                     for t in range(jj + 1, NB):
                         at = t * B - low
                         left = (xs[0][:, at : at + B], xs[1][:, at : at + B])
                         right = (xs[0][:, at:], xs[1][:, at:])
                         uu[t * B : t * B + B, t * B :] -= dot3(left, right, 0, 0)
-                    if jj in (1, 3, 5):
-                        cols_in.run_all((jj + 1) // 2)
 
             return carry
 
         lax.fori_loop(0, NB, body, 0)
+        for stage in (1, 2, 3):
+            cols_in.run_all(stage)
+        gram_first()
         cols_in.from_core()
-        gram_first()
         gram_part(0, NP)
         for jj in range(NB):
-            for copy, _ in u_copies(jj)[:3]:
-                copy.wait_send()
+            for copy, cond in u_copies(jj):
+                pl.when(cond)(copy.wait_send)
         for j in range(NB):
             uu[j * B : j * B + B, j * B : j * B + B] = diag[j * B : j * B + B, :]
         m = uu[own_cols, pl.ds(pl.multiple_of(s * ROWS, B), ROWS)]
@@ -509,17 +554,17 @@
         inner = Copies()
         for t in range(BCH + 3):
             if t < BCH:
-                ref = lead_in.part(here.y, here.zl, t)
-                arrived(ref, one_recv.at[t])
-                for i, (to, cond) in enumerate(here.tree()):
-                    if i != 2:
-                        inner.send(ref, ref, one_send.at[i, t], one_recv.at[t], to, p, cond)
+                pl.when(level > 1)(functools.partial(set_in, t))
+                set_out(inner, level > 1, t)
             for stage in range(4):
                 if 0 <= t - stage < BCH:
                     lead_in.run(stage, t - stage)
             if t == 1:
                 turned()
                 cols_in.run_all(0)
+            if t == 3:
+                cols_in.run_all(1)
+        cols_in.run_all(2)
         lead_in.from_core()
         lead[...] = jnp.zeros_like(lead)
 
@@ -530,40 +575,54 @@
             lead[...] += dot1(jw[...], jr[...])
             return carry
 
-        cols_in.run_all(1)
+        groups = ((0, 1, 2), (3,), (4,), (5, 6), (7,), (8,), (9,))
+
+        def pass_on(jj):
+            arrived(u_rows(jj, c), u_recv.at[jj])
+            for copy, cond in u_copies(jj):
+                pl.when(cond)(copy.start)
+            u_across(jj).start()
+
+        def pass_groups(r):
+            for depth in range(4):
+                if 0 <= r - depth < len(groups):
+
+                    @pl.when(level == depth + 1)
+                    def _():
+                        for jj in groups[r - depth]:
+                            pass_on(jj)
+
+        def substitute(r):
+            for jj in groups[r]:
+                arrived(u_rows(jj, 1 - c), u_core_recv.at[jj])
+                rows = slice(jj * B, jj * B + B)
+                done = dot3(split(uu[rows, rows]), split(lead[rows, :]), 1, 0)
+                lead[rows, :] = done
+                if jj < NB - 1:
+                    low = (jj + 1) * B
+                    lead[low:, :] -= dot3(split(uu[rows, low:]), split(done), 0, 0)
+
+        pass_groups(0)
         lax.fori_loop(0, NP // 2, add, 0)
-        cols_in.run_all(2)
+        pass_groups(1)
+        cols_in.run_all(3)
         lax.fori_loop(NP // 2, NP, add, 0)
-        cols_in.run_all(3)
+        pass_groups(2)
         gram_first()
-        for jj in range(NB):
-            if jj in (3, 6):
-                if jj == 3:
-                    cols_in.from_core()
-                gram_part(0 if jj == 3 else NP // 2, NP // 2 if jj == 3 else NP)
-            arrived(u_rows(jj, c), u_recv.at[jj])
-            for i, (copy, cond) in enumerate(u_copies(jj)):
-                if i != 2:
-                    pl.when(cond)(copy.start)
-            u_across(jj).start()
-            arrived(u_rows(jj, 1 - c), u_core_recv.at[jj])
-            rows = slice(jj * B, jj * B + B)
-            done = dot3(split(uu[rows, rows]), split(lead[rows, :]), 1, 0)
-            lead[rows, :] = done
-            if jj < NB - 1:
-                halves = split(done)
-
-                def minus(t, carry):
-                    at = pl.ds(pl.multiple_of(t * B, B), B)
-                    lead[at, :] -= dot3(split(uu[rows, at]), halves, 0, 0)
-                    return carry
-
-                lax.fori_loop(jj + 1, NB, minus, 0)
+        cols_in.from_core()
+        gram_part(0, NP // 2)
+        pass_groups(3)
+        substitute(0)
+        pass_groups(4)
+        substitute(1)
+        gram_part(NP // 2, NP)
+        for r in range(5, 10):
+            pass_groups(r)
+            substitute(r - 3)
         panel[...] = lead[own_cols, :]
         for jj in range(NB):
-            for i, (copy, cond) in enumerate(u_copies(jj)):
-                if i != 2:
-                    pl.when(cond)(copy.wait_send)
+            for copy, cond in u_copies(jj):
+                pl.when(cond)(copy.wait_send)
             u_across(jj).wait_send()
         lead_in.drain()
         inner.drain()
@@ -588,7 +647,7 @@
     dma, vm = pltpu.SemaphoreType.DMA, pltpu.VMEM
 
     def gather_sems(pieces):
-        return [dma((7, pieces)), dma((7, pieces)), dma((8, pieces)), dma((8, pieces))]
+        return [dma((11, pieces)), dma((7, pieces)), dma((8, pieces)), dma((8, pieces))]
 
     gram, panel = pl.pallas_call(
         mega_kernel,
@@ -609,10 +668,9 @@
             vm((WIDE, 2 * COLS), BF),
             vm((8, COLS), F32),
             vm((NS, 8, COLS), F32),
-            vm((NS, 8, ROWS), F32),
+            vm((NS, 2, ROWS), BF),
             vm((8, COLS), F32),
             vm((NP, 8, COLS), F32),
-            vm((8, ROWS), F32),
             vm((ROWS, 8), F32),
             vm((2, ROWS, 8), F32),
             vm((2, ROWS, 8), F32),

time: 178 us -> 150 us (0.84)
  the two profiles are of different devices: /device:TPU:21 before, /device:TPU:77 now
where the time goes in v5:
time: 150 us; the launch traced here: 149 us
  Pallas kernels  144 us (96%)
  local copies, waits for them, and re-layouts  4.65 us (3%)
    pallas_call x1, Pallas kernels, per_device(): pl.pallas_call(mega_kernel, name='gram_and_panels', out_shape=(jax.ShapeD...  144 us
    unnamed x4, local copies, waits for them, and re-layouts  4.65 us

profile of v5, /device:TPU:77, one launch (start us, length us, event | category | flops | bytes accessed | tf_op | source)
XLA Modules:
  0.0 148.9 jit_solution(7790404173578504256)
XLA Ops:
  0.6 143.6 %gram_and_panels.1 = (f32[640,1280]{1,0:T(8,128)}, f32[160,640]{1,0:T(8,128)}) custom-call(bf16[640,256]{1,0:T(8,128)(2,1)} %act.1, bf16[2,640]{1,0:T(2,128)(2,1)} %bitcast.3), custom_call_target="tpu_custom_call" | custom-call | tf_op jit(solution)/shard_map/gram_and_panels/pallas_call | solution.py:652
  144.3 0.0 copy-start
  144.3 3.9 %copy.6 = f32[640,1280]{1,0:T(8,128)} copy(f32[640,1280]{1,0:T(8,128)} %get-tuple-element.8) | data formatting | bytes 6553600
  148.2 0.0 copy-done
  148.2 0.8 copy.7
Async XLA Ops:
  144.3 3.9 %copy-start = (f32[160,640]{1,0:T(8,128)S(1)}, f32[160,640]{1,0:T(8,128)}, u32[]{:S(2)}) copy-start(f32[160,640]{1,0:T(8,128)} %get-tuple-element.5) | copy-start | bytes 1228804

commit v6 on v5

--- a/solution.py
+++ b/solution.py
@@ -166,7 +166,7 @@
         x, zh, c = self.x, self.zh, self.c
         root = jnp.where(zh == 0, 0, c)
         turn = lax.rem(x - root + NX, NX)
-        side = jnp.where(c == 0, turn == 1, turn == 3)
+        side = jnp.where(c == zh, turn == 1, turn == 3)
         return [
             (self.samp_of(zh, lax.rem(root + 1, NX)), turn == 0),
             (self.samp_of(zh, lax.rem(root + 3, NX)), turn == 0),
@@ -386,9 +386,6 @@
         (c_two_send, c_two_recv, c_core_send, c_core_recv), by_ring=True, busy=k == 0,
     )
 
-    def turn_away(cond):
-        net.send(act, ac.at[c, p], t_send, t_recv, 2 * p + c, k, jnp.logical_and(cond, k != p))
-
     def turned():
         @pl.when(k == p)
         def _():
@@ -423,8 +420,6 @@
             for i in range(1, NS):
                 net.send(mom, moms.at[s], mom_send.at[i], mom_recv.at[s], lax.rem(s + i, NS), p)
             moms[s] = mom[...]
-        if t == 1:
-            turn_away(k > 0)
         if t == 3:
             for i in range(1, NS):
                 j = lax.rem(s + i, NS)
@@ -437,7 +432,7 @@
                 net.send(stat, stats.at[p], stat_send.at[i], stat_recv.at[p], s, lax.rem(p + i, NP))
             stats[p] = stat[...]
 
-    turn_away(k == 0)
+    net.send(act, ac.at[c, p], t_send, t_recv, 2 * p + c, k, k != p)
 
     @pl.when(level == 1)
     def _():
@@ -616,9 +611,21 @@
         pass_groups(4)
         substitute(1)
         gram_part(NP // 2, NP)
-        for r in range(5, 10):
-            pass_groups(r)
-            substitute(r - 3)
+        for depth in range(4):
+
+            @pl.when(level == depth + 1)
+            def _():
+                for r in range(5 - depth, 5):
+                    for jj in groups[r]:
+                        pass_on(jj)
+
+        substitute(2)
+        substitute(3)
+        pass_on(NB - 2)
+        substitute(4)
+        pass_on(NB - 1)
+        substitute(5)
+        substitute(6)
         panel[...] = lead[own_cols, :]
         for jj in range(NB):
             for copy, cond in u_copies(jj):

time: 150 us -> 144 us (0.960)
  Pallas kernels: 144 us -> 139 us
    pallas_call x1, Pallas kernels: 144 us -> 139 us  [per_device(): pl.pallas_call(mega_kernel, name='gram_and_panels', out_shape=(jax.ShapeD...]
where the time goes in v6:
time: 144 us
  Pallas kernels  139 us (97%)
  local copies, waits for them, and re-layouts  4.65 us (3%)
    pallas_call x1, Pallas kernels, per_device(): pl.pallas_call(mega_kernel, name='gram_and_panels', out_shape=(jax.ShapeD...  139 us
    unnamed x4, local copies, waits for them, and re-layouts  4.65 us

profile of v6, /device:TPU:77, one launch (start us, length us, event | category | flops | bytes accessed | tf_op | source)
XLA Modules:
  0.0 144.0 jit_solution(12190362126114901675)
XLA Ops:
  0.6 138.7 %gram_and_panels.1 = (f32[640,1280]{1,0:T(8,128)}, f32[160,640]{1,0:T(8,128)}) custom-call(bf16[640,256]{1,0:T(8,128)(2,1)} %act.1, bf16[2,640]{1,0:T(2,128)(2,1)} %bitcast.3), custom_call_target="tpu_custom_call" | custom-call | tf_op jit(solution)/shard_map/gram_and_panels/pallas_call | solution.py:659
  139.4 0.0 copy-start
  139.4 3.9 %copy.6 = f32[640,1280]{1,0:T(8,128)} copy(f32[640,1280]{1,0:T(8,128)} %get-tuple-element.8) | data formatting | bytes 6553600
  143.3 0.0 copy-done
  143.3 0.8 copy.7
Async XLA Ops:
  139.4 3.9 %copy-start = (f32[160,640]{1,0:T(8,128)S(1)}, f32[160,640]{1,0:T(8,128)}, u32[]{:S(2)}) copy-start(f32[160,640]{1,0:T(8,128)} %get-tuple-element.5) | copy-start | bytes 1228804

commit v7 on v6

--- a/solution.py
+++ b/solution.py
@@ -21,7 +21,7 @@
 ROWS = 640
 COLS = 256
 WIDE = 2 * ROWS
-CH = 4
+CH = 2
 BCH = 2
 NB = 10
 B = 128
@@ -688,7 +688,7 @@
             dma((NS,)), dma((NS,)), dma((NS,)), dma((NS,)), dma((NP,)), dma((NP,)),
         ],
         compiler_params=pltpu.CompilerParams(
-            collective_id=0, has_side_effects=True, vmem_limit_bytes=60 * 2**20
+            collective_id=0, has_side_effects=True, vmem_limit_bytes=48 * 2**20
         ),
     )(activations, signal.T)
     return gram, panel.T

time: 144 us -> 143 us (level)
  Pallas kernels: 139 us -> 137 us
    pallas_call x1, Pallas kernels: 139 us -> 137 us  [per_device(): pl.pallas_call(mega_kernel, name='gram_and_panels', out_shape=(jax.ShapeD...]
    unnamed x4 -> x6, local copies, waits for them, and re-layouts: 4.65 us -> 4.11 us
where the time goes in v7:
time: 143 us; the launch traced here: 142 us
  Pallas kernels  137 us (96%)
  local copies, waits for them, and re-layouts  4.11 us (3%)
    pallas_call x1, Pallas kernels, per_device(): pl.pallas_call(mega_kernel, name='gram_and_panels', out_shape=(jax.ShapeD...  137 us
    unnamed x6, local copies, waits for them, and re-layouts  4.11 us

profile of v7, /device:TPU:77, one launch (start us, length us, event | category | flops | bytes accessed | tf_op | source)
XLA Modules:
  0.0 142.0 jit_solution(11751648072697921908)
XLA Ops:
  0.6 0.0 copy-start
  0.6 1.0 copy-done
  1.6 0.0 copy-start.1
  1.6 0.7 copy-done.1
  2.3 137.3 %gram_and_panels.1 = (f32[640,1280]{1,0:T(8,128)S(1)}, f32[160,640]{1,0:T(8,128)S(1)}) custom-call(bf16[640,256]{1,0:T(8,128)(2,1)S(1)} %copy-done, bf16[2,640]{1,0:T(2,128)(2,1)S(1)} %bitcast.3), custom_call_target="tpu_custom_call" | custom-call | tf_op jit(solution)/shard_map/gram_and_panels/pallas_call | solution.py:659
  139.6 1.7 %copy.6 = f32[640,1280]{1,0:T(8,128)} copy(f32[640,1280]{1,0:T(8,128)S(1)} %get-tuple-element.8) | data formatting | bytes 6553600
  141.3 0.8 copy.7
Async XLA Ops:
  0.6 1.0 copy-start
  1.6 0.7 copy-start.1
